TPU v7x, 512 devices: a whole 4x4x16 slice. The times are simulated.
512 devices in a mesh: blk: 32 (over z, y_lo), sub: 16 (over x, y_hi, core).
Axes of the slice: x: 4, y: 4 (y_hi: 2, y_lo: 2; y = y_hi * 2 + y_lo), z: 16, core: 2. Of those that a mesh axis runs over, the one named last changes fastest.
Arguments:
- rhs_interior: bfloat16 [4096, 16, 2, 128], P(('blk', 'sub')), may hold values from -6 to 6
- block_inverse: bfloat16 [4096, 2, 128, 128], P(('blk', 'sub')), may hold values from -0.5 to 0.5
- rhs_interface: float32 [16, 262144], P(None, ('blk', 'sub')), may hold values from -6 to 6
- band_cells: int32 [5, 262144], P(None, ('blk', 'sub')), may hold values from 0 to 255
- band_weights: float32 [5, 262144], P(None, ('blk', 'sub')), may hold values from -4 to 4
- group_map: int32 [32, 8192], P('blk'), may hold values from 0 to 4095, as said below
- schur_slab: float32 [2048, 131072], P('blk', 'sub'), may hold values from -0.03125 to 0.03125
Outputs:
- interior_update: float32 [4096, 16, 2, 128], P(('blk', 'sub'))
- slab_residual: float32 [16, 2048], P(None, ('blk', 'sub'))
Inputs may be any that keep to these rules, and one draw needn't show every extreme that they name: `group_map`: within a row block, the rows of each device name each owner index exactly 512 / 16 times, and every assembled unknown of the block is named by exactly two rows.
All inputs are finite; a program needn't handle non-finite values.
Results may differ from a plain program's by a relative error of at most 0.0028.
Values sent between devices are 32-bit elements; how exact they have to be, the bound alone decides.
No kernel may reach another device: no remote copies, remote signals or barrier semaphores. Data moves between devices by JAX's collectives and lax.ppermute only.
A program may use at most 64 MiB of HBM per device.

v0:
```python
import jax
import jax.numpy as jnp
from jax import lax
from jax.sharding import PartitionSpec as P


def passed_along(value, axis, by):
    peers = lax.axis_size(axis)
    return lax.ppermute(value, axis, [(i, (i + by) % peers) for i in range(peers)])


def apply_blocks(values, inverses):
    return jnp.einsum("dsbk,dbjk->dsbj", values, inverses, preferred_element_type=jnp.float32)


def per_device(
    rhs_interior, block_inverse, rhs_interface, band_cells, band_weights, group_map, schur_slab
):
    spread = lax.axis_size("sub")
    cycle_size = lax.axis_size("blk")
    sub_count, species, blocks, block_cells = rhs_interior.shape
    cell_count = blocks * block_cells
    local_rows = rhs_interface.shape[1]
    face_rows = local_rows // sub_count
    slot_count = local_rows // 2
    per_peer = local_rows // spread
    interior = apply_blocks(rhs_interior, block_inverse)
    flat_cells = jnp.transpose(interior.reshape(sub_count, species, cell_count), (1, 0, 2)).reshape(
        species, sub_count * cell_count
    )
    row_ids = jnp.arange(local_rows, dtype=jnp.int32)
    cell_index = (row_ids // face_rows)[None, :] * cell_count + band_cells
    picked = flat_cells[:, cell_index]
    face_values = rhs_interface - jnp.sum(band_weights[None] * picked, axis=1)
    mapped = group_map[0].reshape(spread, local_rows)
    target = mapped // slot_count
    placed = mapped % slot_count
    onehot = (target[:, :, None] == jnp.arange(spread, dtype=jnp.int32)[None, None, :]).astype(
        jnp.int32
    )
    rank_in = jnp.sum(onehot * (jnp.cumsum(onehot, axis=1) - 1), axis=2)
    own_index = lax.axis_index("sub")
    send_slot = target[own_index] * per_peer + rank_in[own_index]
    outgoing = jnp.zeros_like(face_values).at[:, send_slot].set(face_values)
    incoming = lax.all_to_all(outgoing, "sub", split_axis=1, concat_axis=1, tiled=True)
    arrival = jnp.arange(spread, dtype=jnp.int32)[:, None] * per_peer + rank_in
    landing = jnp.where(target == own_index, arrival, local_rows)
    slot_of = (
        jnp.zeros((local_rows,), jnp.int32)
        .at[landing.reshape(-1)]
        .set(placed.reshape(-1), mode="drop")
    )
    assembled = jnp.zeros((species, slot_count), jnp.float32).at[:, slot_of].add(incoming)
    blk_index = lax.axis_index("blk")

    def panel_term(panel_now, source):
        columns = lax.dynamic_slice_in_dim(schur_slab, source * slot_count, slot_count, 1)
        return lax.dot_general(
            panel_now,
            columns,
            (((1,), (1,)), ((), ())),
            precision=lax.Precision.HIGHEST,
            preferred_element_type=jnp.float32,
        )

    def advance(turn_index, carry):
        panel_now, running = carry
        panel_now = passed_along(panel_now, "blk", 1)
        return (panel_now, running + panel_term(panel_now, (blk_index - turn_index) % cycle_size))

    final_panel, partial_value = lax.fori_loop(
        1, cycle_size, advance, (assembled, panel_term(assembled, blk_index))
    )
    own_rows = lax.psum_scatter(partial_value, "sub", scatter_dimension=1, tiled=True)
    slab_residual = assembled[:, : own_rows.shape[1]] - own_rows
    back_values = lax.all_to_all(
        assembled[:, slot_of], "sub", split_axis=1, concat_axis=1, tiled=True
    )
    row_values = back_values[:, send_slot]
    contrib = (band_weights[None] * row_values[:, None, :]).reshape(species, -1)
    correction = (
        jnp.zeros((species, sub_count * cell_count), jnp.float32)
        .at[:, cell_index.reshape(-1)]
        .add(contrib)
    )
    correction = jnp.transpose(
        correction.reshape(species, sub_count, blocks, block_cells), (1, 0, 2, 3)
    )
    reduced = (rhs_interior.astype(jnp.float32) - correction).astype(jnp.bfloat16)
    interior_update = apply_blocks(reduced, block_inverse)
    return (interior_update, slab_residual)


def solution(mesh):
    placed = (
        P(("blk", "sub"), None, None, None),
        P(("blk", "sub"), None, None, None),
        P(None, ("blk", "sub")),
        P(None, ("blk", "sub")),
        P(None, ("blk", "sub")),
        P("blk", None),
        P("blk", "sub"),
    )
    return jax.shard_map(
        per_device,
        mesh=mesh,
        in_specs=placed,
        out_specs=(P(("blk", "sub"), None, None, None), P(None, ("blk", "sub"))),
        check_vma=False,
    )
```

profile of v0, /device:TPU:1, one launch (start us, length us, event | category | flops | bytes accessed | tf_op | source)
XLA Modules:
  0.0 450.1 jit_solution(185135858513748457)
XLA Ops:
  1.6 18.1 %reduce-window.6 = s32[16,16,4,128]{3,1,2,0:T(8,128)S(1)} reduce-window(s32[16,16,4,128]{3,1,2,0:T(8,128)S(1)} %fusion.8, s32[]{:T(128)} %constant.134.clone.1), window={size=1x1x1x128 pad=0_0x0_0x0_0x127_0}, to_apply=%region_0.1 | reduce-window | flops 16646144 | bytes 1048580 | tf_op jit(solution)/shard_map/reduce-window
  23.1 4.2 gather_fusion
  30.3 10.1 %all-to-all-start = ((f32[16,1,512]{2,1,0:T(1,128)}), f32[16,1,512]{2,1,0:T(1,128)S(1)}, u32[]{:S(2)}, u32[]{:S(2)}) async-start(f32[16,1,512]{2,1,0:T(1,128)} %reshape.350), calls=%async_computation | async-start | bytes 65536 | tf_op jit(solution)/shard_map/all_to_all | solution.py:45
  40.8 30.4 %scatter_custom_fusion = s32[512]{0:T(512)S(1)} fusion(s32[8192]{0:T(1024)S(1)} %bitcast.116, s32[8192]{0:T(1024)S(1)} %add_select_fusion, s32[]{:T(128)} %constant.134.clone.1), kind=kCustom, calls=%fused_computation.84 | custom fusion | bytes 2052 | tf_op jit(solution)/shard_map/scatter | solution.py:51
  74.7 2.3 scatter_custom_fusion.2
  78.2 240.1 %while.17 = (s32[]{:T(128)}, f32[16,256]{1,0:T(8,128)S(1)}, f32[16,64]{1,0:T(8,128)S(1)}, s32[]{:T(128)}, f32[64,8192]{1,0:T(8,128)}, /*index=5*/s32[]{:T(128)},...) while((s32[]{:T(128)}, f32[16,256]{1,0:T(8,128)S(1)}, f32[16,64]{1,0:T(8,128)S(1)}, ...), condition=%wide.region_9.10_spmd, body=%wide.region_8.9_spmd.sunk | while | flops 3146770 | bytes 188736 | solution.py:71
  78.2 2.0 collective-permute-start
  80.2 8.7 %collective-permute-done = f32[16,256]{1,0:T(8,128)S(1)} collective-permute-done((f32[16,256]{1,0:T(8,128)S(1)}, f32[16,256]{1,0:T(8,128)S(1)}, u32[]{:S(2)}, u32[]{:S(2)}) %collective-permute-start) | collective-permute-done | bytes 16416 | tf_op jit(solution)/shard_map/while/body/eval_jaxpr/ppermute | solution.py:9
  89.9 1.9 collective-permute-start
  91.9 4.6 %collective-permute-done = f32[16,256]{1,0:T(8,128)S(1)} collective-permute-done((f32[16,256]{1,0:T(8,128)S(1)}, f32[16,256]{1,0:T(8,128)S(1)}, u32[]{:S(2)}, u32[]{:S(2)}) %collective-permute-start) | collective-permute-done | bytes 16416 | tf_op jit(solution)/shard_map/while/body/eval_jaxpr/ppermute | solution.py:9
  97.5 1.9 collective-permute-start
  99.5 4.6 %collective-permute-done = f32[16,256]{1,0:T(8,128)S(1)} collective-permute-done((f32[16,256]{1,0:T(8,128)S(1)}, f32[16,256]{1,0:T(8,128)S(1)}, u32[]{:S(2)}, u32[]{:S(2)}) %collective-permute-start) | collective-permute-done | bytes 16416 | tf_op jit(solution)/shard_map/while/body/eval_jaxpr/ppermute | solution.py:9
  105.1 1.9 collective-permute-start
  107.1 4.6 %collective-permute-done = f32[16,256]{1,0:T(8,128)S(1)} collective-permute-done((f32[16,256]{1,0:T(8,128)S(1)}, f32[16,256]{1,0:T(8,128)S(1)}, u32[]{:S(2)}, u32[]{:S(2)}) %collective-permute-start) | collective-permute-done | bytes 16416 | tf_op jit(solution)/shard_map/while/body/eval_jaxpr/ppermute | solution.py:9
  112.7 1.9 collective-permute-start
  114.7 4.6 %collective-permute-done = f32[16,256]{1,0:T(8,128)S(1)} collective-permute-done((f32[16,256]{1,0:T(8,128)S(1)}, f32[16,256]{1,0:T(8,128)S(1)}, u32[]{:S(2)}, u32[]{:S(2)}) %collective-permute-start) | collective-permute-done | bytes 16416 | tf_op jit(solution)/shard_map/while/body/eval_jaxpr/ppermute | solution.py:9
  120.3 1.9 collective-permute-start
  122.3 4.6 %collective-permute-done = f32[16,256]{1,0:T(8,128)S(1)} collective-permute-done((f32[16,256]{1,0:T(8,128)S(1)}, f32[16,256]{1,0:T(8,128)S(1)}, u32[]{:S(2)}, u32[]{:S(2)}) %collective-permute-start) | collective-permute-done | bytes 16416 | tf_op jit(solution)/shard_map/while/body/eval_jaxpr/ppermute | solution.py:9
  127.9 1.9 collective-permute-start
  129.9 4.6 %collective-permute-done = f32[16,256]{1,0:T(8,128)S(1)} collective-permute-done((f32[16,256]{1,0:T(8,128)S(1)}, f32[16,256]{1,0:T(8,128)S(1)}, u32[]{:S(2)}, u32[]{:S(2)}) %collective-permute-start) | collective-permute-done | bytes 16416 | tf_op jit(solution)/shard_map/while/body/eval_jaxpr/ppermute | solution.py:9
  135.5 1.9 collective-permute-start
  137.5 4.6 %collective-permute-done = f32[16,256]{1,0:T(8,128)S(1)} collective-permute-done((f32[16,256]{1,0:T(8,128)S(1)}, f32[16,256]{1,0:T(8,128)S(1)}, u32[]{:S(2)}, u32[]{:S(2)}) %collective-permute-start) | collective-permute-done | bytes 16416 | tf_op jit(solution)/shard_map/while/body/eval_jaxpr/ppermute | solution.py:9
  143.1 1.9 collective-permute-start
  145.1 4.6 %collective-permute-done = f32[16,256]{1,0:T(8,128)S(1)} collective-permute-done((f32[16,256]{1,0:T(8,128)S(1)}, f32[16,256]{1,0:T(8,128)S(1)}, u32[]{:S(2)}, u32[]{:S(2)}) %collective-permute-start) | collective-permute-done | bytes 16416 | tf_op jit(solution)/shard_map/while/body/eval_jaxpr/ppermute | solution.py:9
  150.7 1.9 collective-permute-start
  152.7 4.6 %collective-permute-done = f32[16,256]{1,0:T(8,128)S(1)} collective-permute-done((f32[16,256]{1,0:T(8,128)S(1)}, f32[16,256]{1,0:T(8,128)S(1)}, u32[]{:S(2)}, u32[]{:S(2)}) %collective-permute-start) | collective-permute-done | bytes 16416 | tf_op jit(solution)/shard_map/while/body/eval_jaxpr/ppermute | solution.py:9
  158.3 1.9 collective-permute-start
  160.3 4.6 %collective-permute-done = f32[16,256]{1,0:T(8,128)S(1)} collective-permute-done((f32[16,256]{1,0:T(8,128)S(1)}, f32[16,256]{1,0:T(8,128)S(1)}, u32[]{:S(2)}, u32[]{:S(2)}) %collective-permute-start) | collective-permute-done | bytes 16416 | tf_op jit(solution)/shard_map/while/body/eval_jaxpr/ppermute | solution.py:9
  165.9 1.9 collective-permute-start
  167.9 4.6 %collective-permute-done = f32[16,256]{1,0:T(8,128)S(1)} collective-permute-done((f32[16,256]{1,0:T(8,128)S(1)}, f32[16,256]{1,0:T(8,128)S(1)}, u32[]{:S(2)}, u32[]{:S(2)}) %collective-permute-start) | collective-permute-done | bytes 16416 | tf_op jit(solution)/shard_map/while/body/eval_jaxpr/ppermute | solution.py:9
  173.5 1.9 collective-permute-start
  175.5 4.6 %collective-permute-done = f32[16,256]{1,0:T(8,128)S(1)} collective-permute-done((f32[16,256]{1,0:T(8,128)S(1)}, f32[16,256]{1,0:T(8,128)S(1)}, u32[]{:S(2)}, u32[]{:S(2)}) %collective-permute-start) | collective-permute-done | bytes 16416 | tf_op jit(solution)/shard_map/while/body/eval_jaxpr/ppermute | solution.py:9
  181.1 1.9 collective-permute-start
  183.1 4.6 %collective-permute-done = f32[16,256]{1,0:T(8,128)S(1)} collective-permute-done((f32[16,256]{1,0:T(8,128)S(1)}, f32[16,256]{1,0:T(8,128)S(1)}, u32[]{:S(2)}, u32[]{:S(2)}) %collective-permute-start) | collective-permute-done | bytes 16416 | tf_op jit(solution)/shard_map/while/body/eval_jaxpr/ppermute | solution.py:9
  188.7 1.9 collective-permute-start
  190.7 4.6 %collective-permute-done = f32[16,256]{1,0:T(8,128)S(1)} collective-permute-done((f32[16,256]{1,0:T(8,128)S(1)}, f32[16,256]{1,0:T(8,128)S(1)}, u32[]{:S(2)}, u32[]{:S(2)}) %collective-permute-start) | collective-permute-done | bytes 16416 | tf_op jit(solution)/shard_map/while/body/eval_jaxpr/ppermute | solution.py:9
  196.3 1.9 collective-permute-start
  198.3 5.1 %collective-permute-done = f32[16,256]{1,0:T(8,128)S(1)} collective-permute-done((f32[16,256]{1,0:T(8,128)S(1)}, f32[16,256]{1,0:T(8,128)S(1)}, u32[]{:S(2)}, u32[]{:S(2)}) %collective-permute-start) | collective-permute-done | bytes 16416 | tf_op jit(solution)/shard_map/while/body/eval_jaxpr/ppermute | solution.py:9
  204.4 1.9 collective-permute-start
  206.3 4.6 %collective-permute-done = f32[16,256]{1,0:T(8,128)S(1)} collective-permute-done((f32[16,256]{1,0:T(8,128)S(1)}, f32[16,256]{1,0:T(8,128)S(1)}, u32[]{:S(2)}, u32[]{:S(2)}) %collective-permute-start) | collective-permute-done | bytes 16416 | tf_op jit(solution)/shard_map/while/body/eval_jaxpr/ppermute | solution.py:9
  212.0 1.9 collective-permute-start
  213.9 4.6 %collective-permute-done = f32[16,256]{1,0:T(8,128)S(1)} collective-permute-done((f32[16,256]{1,0:T(8,128)S(1)}, f32[16,256]{1,0:T(8,128)S(1)}, u32[]{:S(2)}, u32[]{:S(2)}) %collective-permute-start) | collective-permute-done | bytes 16416 | tf_op jit(solution)/shard_map/while/body/eval_jaxpr/ppermute | solution.py:9
  219.5 1.9 collective-permute-start
  221.5 4.6 %collective-permute-done = f32[16,256]{1,0:T(8,128)S(1)} collective-permute-done((f32[16,256]{1,0:T(8,128)S(1)}, f32[16,256]{1,0:T(8,128)S(1)}, u32[]{:S(2)}, u32[]{:S(2)}) %collective-permute-start) | collective-permute-done | bytes 16416 | tf_op jit(solution)/shard_map/while/body/eval_jaxpr/ppermute | solution.py:9
  227.1 1.9 collective-permute-start
  229.1 4.6 %collective-permute-done = f32[16,256]{1,0:T(8,128)S(1)} collective-permute-done((f32[16,256]{1,0:T(8,128)S(1)}, f32[16,256]{1,0:T(8,128)S(1)}, u32[]{:S(2)}, u32[]{:S(2)}) %collective-permute-start) | collective-permute-done | bytes 16416 | tf_op jit(solution)/shard_map/while/body/eval_jaxpr/ppermute | solution.py:9
  234.7 1.9 collective-permute-start
  236.7 4.6 %collective-permute-done = f32[16,256]{1,0:T(8,128)S(1)} collective-permute-done((f32[16,256]{1,0:T(8,128)S(1)}, f32[16,256]{1,0:T(8,128)S(1)}, u32[]{:S(2)}, u32[]{:S(2)}) %collective-permute-start) | collective-permute-done | bytes 16416 | tf_op jit(solution)/shard_map/while/body/eval_jaxpr/ppermute | solution.py:9
  244.3 4.6 %collective-permute-done = f32[16,256]{1,0:T(8,128)S(1)} collective-permute-done((f32[16,256]{1,0:T(8,128)S(1)}, f32[16,256]{1,0:T(8,128)S(1)}, u32[]{:S(2)}, u32[]{:S(2)}) %collective-permute-start) | collective-permute-done | bytes 16416 | tf_op jit(solution)/shard_map/while/body/eval_jaxpr/ppermute | solution.py:9
  249.9 1.9 collective-permute-start
  251.9 4.6 %collective-permute-done = f32[16,256]{1,0:T(8,128)S(1)} collective-permute-done((f32[16,256]{1,0:T(8,128)S(1)}, f32[16,256]{1,0:T(8,128)S(1)}, u32[]{:S(2)}, u32[]{:S(2)}) %collective-permute-start) | collective-permute-done | bytes 16416 | tf_op jit(solution)/shard_map/while/body/eval_jaxpr/ppermute | solution.py:9
  259.5 4.6 %collective-permute-done = f32[16,256]{1,0:T(8,128)S(1)} collective-permute-done((f32[16,256]{1,0:T(8,128)S(1)}, f32[16,256]{1,0:T(8,128)S(1)}, u32[]{:S(2)}, u32[]{:S(2)}) %collective-permute-start) | collective-permute-done | bytes 16416 | tf_op jit(solution)/shard_map/while/body/eval_jaxpr/ppermute | solution.py:9
  267.1 4.6 %collective-permute-done = f32[16,256]{1,0:T(8,128)S(1)} collective-permute-done((f32[16,256]{1,0:T(8,128)S(1)}, f32[16,256]{1,0:T(8,128)S(1)}, u32[]{:S(2)}, u32[]{:S(2)}) %collective-permute-start) | collective-permute-done | bytes 16416 | tf_op jit(solution)/shard_map/while/body/eval_jaxpr/ppermute | solution.py:9
  274.7 4.6 %collective-permute-done = f32[16,256]{1,0:T(8,128)S(1)} collective-permute-done((f32[16,256]{1,0:T(8,128)S(1)}, f32[16,256]{1,0:T(8,128)S(1)}, u32[]{:S(2)}, u32[]{:S(2)}) %collective-permute-start) | collective-permute-done | bytes 16416 | tf_op jit(solution)/shard_map/while/body/eval_jaxpr/ppermute | solution.py:9
  280.3 1.9 collective-permute-start
  282.3 4.6 %collective-permute-done = f32[16,256]{1,0:T(8,128)S(1)} collective-permute-done((f32[16,256]{1,0:T(8,128)S(1)}, f32[16,256]{1,0:T(8,128)S(1)}, u32[]{:S(2)}, u32[]{:S(2)}) %collective-permute-start) | collective-permute-done | bytes 16416 | tf_op jit(solution)/shard_map/while/body/eval_jaxpr/ppermute | solution.py:9
  289.9 4.6 %collective-permute-done = f32[16,256]{1,0:T(8,128)S(1)} collective-permute-done((f32[16,256]{1,0:T(8,128)S(1)}, f32[16,256]{1,0:T(8,128)S(1)}, u32[]{:S(2)}, u32[]{:S(2)}) %collective-permute-start) | collective-permute-done | bytes 16416 | tf_op jit(solution)/shard_map/while/body/eval_jaxpr/ppermute | solution.py:9
  297.5 4.6 %collective-permute-done = f32[16,256]{1,0:T(8,128)S(1)} collective-permute-done((f32[16,256]{1,0:T(8,128)S(1)}, f32[16,256]{1,0:T(8,128)S(1)}, u32[]{:S(2)}, u32[]{:S(2)}) %collective-permute-start) | collective-permute-done | bytes 16416 | tf_op jit(solution)/shard_map/while/body/eval_jaxpr/ppermute | solution.py:9
  305.1 4.6 %collective-permute-done = f32[16,256]{1,0:T(8,128)S(1)} collective-permute-done((f32[16,256]{1,0:T(8,128)S(1)}, f32[16,256]{1,0:T(8,128)S(1)}, u32[]{:S(2)}, u32[]{:S(2)}) %collective-permute-start) | collective-permute-done | bytes 16416 | tf_op jit(solution)/shard_map/while/body/eval_jaxpr/ppermute | solution.py:9
  312.7 4.6 %collective-permute-done = f32[16,256]{1,0:T(8,128)S(1)} collective-permute-done((f32[16,256]{1,0:T(8,128)S(1)}, f32[16,256]{1,0:T(8,128)S(1)}, u32[]{:S(2)}, u32[]{:S(2)}) %collective-permute-start) | collective-permute-done | bytes 16416 | tf_op jit(solution)/shard_map/while/body/eval_jaxpr/ppermute | solution.py:9
  318.4 94.9 %all-reduce = f32[16,64]{0,1:T(8,128)S(1)} all-reduce(f32[16,64]{0,1:T(8,128)S(1)} %copy.58), channel_id=2, replica_groups=mesh['blk'=32,'sub'=16] {'sub'}, use_global_device_ids=true, to_apply=%region_10.11.clone | all-reduce | flops 1024 | bytes 8192
  415.2 9.2 %all-to-all-start.1 = ((f32[16,1,512]{2,1,0:T(1,128)}), f32[16,1,512]{2,1,0:T(1,128)S(1)}, u32[]{:S(2)}, u32[]{:S(2)}) async-start(f32[16,1,512]{2,1,0:T(1,128)} %reshape.352), calls=%async_computation.1 | async-start | bytes 65536 | tf_op jit(solution)/shard_map/all_to_all | solution.py:76
  425.0 6.8 %all-to-all-done.1 = f32[16,1,512]{2,1,0:T(1,128)S(1)} async-done(((f32[16,1,512]{2,1,0:T(1,128)}), f32[16,1,512]{2,1,0:T(1,128)S(1)}, u32[]{:S(2)}, u32[]{:S(2)}) %all-to-all-start.1) | async-done | bytes 32800 | tf_op jit(solution)/shard_map/all_to_all | solution.py:76
  434.1 14.5 %scatter_custom_fusion.3 = f32[16,2048]{0,1:T(8,128)S(1)} fusion(s32[2560]{0:T(1024)S(1)} %fusion.26, f32[16,2560]{0,1:T(8,128)S(1)} %bitcast_multiply_fusion, f32[]{:T(128)} %constant.131.clone.1), kind=kCustom, calls=%fused_computation.11 | custom fusion | flops 40960 | bytes 1441796 | tf_op jit(solution)/shard_map/scatter-add | solution.py:84
  (142 shorter events, 63.9 us)
Async XLA Ops:
  0.6 21.3 %copy-start = (bf16[8,2,128,128]{3,2,1,0:T(8,128)(2,1)S(1)}, bf16[8,2,128,128]{3,2,1,0:T(8,128)(2,1)}, u32[]{:S(2)}) copy-start(bf16[8,2,128,128]{3,2,1,0:T(8,128)(2,1)} %param.10) | copy-start | bytes 1572868
  1.6 19.5 %copy-start.1 = (s32[1,8192]{1,0:T(1,128)S(1)}, s32[1,8192]{1,0:T(1,128)}, u32[]{:S(2)}) copy-start(s32[1,8192]{1,0:T(1,128)} %param.14) | copy-start | bytes 98308
  1.6 20.3 %copy-start.5 = (s32[5,512]{1,0:T(8,128)S(1)}, s32[5,512]{1,0:T(8,128)}, u32[]{:S(2)}) copy-start(s32[5,512]{1,0:T(8,128)} %param.12) | copy-start | bytes 30724
  19.7 2.2 copy-start.2
  20.5 2.1 copy-start.4
  23.0 4.2 copy-start.3
  30.3 42.9 %all-to-all-start = ((f32[16,1,512]{2,1,0:T(1,128)}), f32[16,1,512]{2,1,0:T(1,128)S(1)}, u32[]{:S(2)}, u32[]{:S(2)}) async-start(f32[16,1,512]{2,1,0:T(1,128)} %reshape.350), calls=%async_computation | async-start | bytes 65536 | tf_op jit(solution)/shard_map/all_to_all | solution.py:45
  78.2 10.7 %collective-permute-start = (f32[16,256]{1,0:T(8,128)S(1)}, f32[16,256]{1,0:T(8,128)S(1)}, u32[]{:S(2)}, u32[]{:S(2)}) collective-permute-start(f32[16,256]{1,0:T(8,128)S(1)} %get-tuple-element.219), channel_id=1, source_target_pairs={{0,16},{16,32},{32,48},{48,64},{64,80},{80,96},{96,112},{112,128},... | collective-permute-start | bytes 49160 | tf_op jit(solution)/shard_map/while/body/eval_jaxpr/ppermute | solution.py:9
  89.9 6.6 %collective-permute-start = (f32[16,256]{1,0:T(8,128)S(1)}, f32[16,256]{1,0:T(8,128)S(1)}, u32[]{:S(2)}, u32[]{:S(2)}) collective-permute-start(f32[16,256]{1,0:T(8,128)S(1)} %get-tuple-element.219), channel_id=1, source_target_pairs={{0,16},{16,32},{32,48},{48,64},{64,80},{80,96},{96,112},{112,128},... | collective-permute-start | bytes 49160 | tf_op jit(solution)/shard_map/while/body/eval_jaxpr/ppermute | solution.py:9
  97.5 6.6 %collective-permute-start = (f32[16,256]{1,0:T(8,128)S(1)}, f32[16,256]{1,0:T(8,128)S(1)}, u32[]{:S(2)}, u32[]{:S(2)}) collective-permute-start(f32[16,256]{1,0:T(8,128)S(1)} %get-tuple-element.219), channel_id=1, source_target_pairs={{0,16},{16,32},{32,48},{48,64},{64,80},{80,96},{96,112},{112,128},... | collective-permute-start | bytes 49160 | tf_op jit(solution)/shard_map/while/body/eval_jaxpr/ppermute | solution.py:9
  105.1 6.6 %collective-permute-start = (f32[16,256]{1,0:T(8,128)S(1)}, f32[16,256]{1,0:T(8,128)S(1)}, u32[]{:S(2)}, u32[]{:S(2)}) collective-permute-start(f32[16,256]{1,0:T(8,128)S(1)} %get-tuple-element.219), channel_id=1, source_target_pairs={{0,16},{16,32},{32,48},{48,64},{64,80},{80,96},{96,112},{112,128},... | collective-permute-start | bytes 49160 | tf_op jit(solution)/shard_map/while/body/eval_jaxpr/ppermute | solution.py:9
  112.7 6.6 %collective-permute-start = (f32[16,256]{1,0:T(8,128)S(1)}, f32[16,256]{1,0:T(8,128)S(1)}, u32[]{:S(2)}, u32[]{:S(2)}) collective-permute-start(f32[16,256]{1,0:T(8,128)S(1)} %get-tuple-element.219), channel_id=1, source_target_pairs={{0,16},{16,32},{32,48},{48,64},{64,80},{80,96},{96,112},{112,128},... | collective-permute-start | bytes 49160 | tf_op jit(solution)/shard_map/while/body/eval_jaxpr/ppermute | solution.py:9
  120.3 6.6 %collective-permute-start = (f32[16,256]{1,0:T(8,128)S(1)}, f32[16,256]{1,0:T(8,128)S(1)}, u32[]{:S(2)}, u32[]{:S(2)}) collective-permute-start(f32[16,256]{1,0:T(8,128)S(1)} %get-tuple-element.219), channel_id=1, source_target_pairs={{0,16},{16,32},{32,48},{48,64},{64,80},{80,96},{96,112},{112,128},... | collective-permute-start | bytes 49160 | tf_op jit(solution)/shard_map/while/body/eval_jaxpr/ppermute | solution.py:9
  127.9 6.6 %collective-permute-start = (f32[16,256]{1,0:T(8,128)S(1)}, f32[16,256]{1,0:T(8,128)S(1)}, u32[]{:S(2)}, u32[]{:S(2)}) collective-permute-start(f32[16,256]{1,0:T(8,128)S(1)} %get-tuple-element.219), channel_id=1, source_target_pairs={{0,16},{16,32},{32,48},{48,64},{64,80},{80,96},{96,112},{112,128},... | collective-permute-start | bytes 49160 | tf_op jit(solution)/shard_map/while/body/eval_jaxpr/ppermute | solution.py:9
  135.5 6.6 %collective-permute-start = (f32[16,256]{1,0:T(8,128)S(1)}, f32[16,256]{1,0:T(8,128)S(1)}, u32[]{:S(2)}, u32[]{:S(2)}) collective-permute-start(f32[16,256]{1,0:T(8,128)S(1)} %get-tuple-element.219), channel_id=1, source_target_pairs={{0,16},{16,32},{32,48},{48,64},{64,80},{80,96},{96,112},{112,128},... | collective-permute-start | bytes 49160 | tf_op jit(solution)/shard_map/while/body/eval_jaxpr/ppermute | solution.py:9
  143.1 6.6 %collective-permute-start = (f32[16,256]{1,0:T(8,128)S(1)}, f32[16,256]{1,0:T(8,128)S(1)}, u32[]{:S(2)}, u32[]{:S(2)}) collective-permute-start(f32[16,256]{1,0:T(8,128)S(1)} %get-tuple-element.219), channel_id=1, source_target_pairs={{0,16},{16,32},{32,48},{48,64},{64,80},{80,96},{96,112},{112,128},... | collective-permute-start | bytes 49160 | tf_op jit(solution)/shard_map/while/body/eval_jaxpr/ppermute | solution.py:9
  150.7 6.6 %collective-permute-start = (f32[16,256]{1,0:T(8,128)S(1)}, f32[16,256]{1,0:T(8,128)S(1)}, u32[]{:S(2)}, u32[]{:S(2)}) collective-permute-start(f32[16,256]{1,0:T(8,128)S(1)} %get-tuple-element.219), channel_id=1, source_target_pairs={{0,16},{16,32},{32,48},{48,64},{64,80},{80,96},{96,112},{112,128},... | collective-permute-start | bytes 49160 | tf_op jit(solution)/shard_map/while/body/eval_jaxpr/ppermute | solution.py:9
  158.3 6.6 %collective-permute-start = (f32[16,256]{1,0:T(8,128)S(1)}, f32[16,256]{1,0:T(8,128)S(1)}, u32[]{:S(2)}, u32[]{:S(2)}) collective-permute-start(f32[16,256]{1,0:T(8,128)S(1)} %get-tuple-element.219), channel_id=1, source_target_pairs={{0,16},{16,32},{32,48},{48,64},{64,80},{80,96},{96,112},{112,128},... | collective-permute-start | bytes 49160 | tf_op jit(solution)/shard_map/while/body/eval_jaxpr/ppermute | solution.py:9
  165.9 6.6 %collective-permute-start = (f32[16,256]{1,0:T(8,128)S(1)}, f32[16,256]{1,0:T(8,128)S(1)}, u32[]{:S(2)}, u32[]{:S(2)}) collective-permute-start(f32[16,256]{1,0:T(8,128)S(1)} %get-tuple-element.219), channel_id=1, source_target_pairs={{0,16},{16,32},{32,48},{48,64},{64,80},{80,96},{96,112},{112,128},... | collective-permute-start | bytes 49160 | tf_op jit(solution)/shard_map/while/body/eval_jaxpr/ppermute | solution.py:9
  173.5 6.6 %collective-permute-start = (f32[16,256]{1,0:T(8,128)S(1)}, f32[16,256]{1,0:T(8,128)S(1)}, u32[]{:S(2)}, u32[]{:S(2)}) collective-permute-start(f32[16,256]{1,0:T(8,128)S(1)} %get-tuple-element.219), channel_id=1, source_target_pairs={{0,16},{16,32},{32,48},{48,64},{64,80},{80,96},{96,112},{112,128},... | collective-permute-start | bytes 49160 | tf_op jit(solution)/shard_map/while/body/eval_jaxpr/ppermute | solution.py:9
  181.1 6.6 %collective-permute-start = (f32[16,256]{1,0:T(8,128)S(1)}, f32[16,256]{1,0:T(8,128)S(1)}, u32[]{:S(2)}, u32[]{:S(2)}) collective-permute-start(f32[16,256]{1,0:T(8,128)S(1)} %get-tuple-element.219), channel_id=1, source_target_pairs={{0,16},{16,32},{32,48},{48,64},{64,80},{80,96},{96,112},{112,128},... | collective-permute-start | bytes 49160 | tf_op jit(solution)/shard_map/while/body/eval_jaxpr/ppermute | solution.py:9
  188.7 6.6 %collective-permute-start = (f32[16,256]{1,0:T(8,128)S(1)}, f32[16,256]{1,0:T(8,128)S(1)}, u32[]{:S(2)}, u32[]{:S(2)}) collective-permute-start(f32[16,256]{1,0:T(8,128)S(1)} %get-tuple-element.219), channel_id=1, source_target_pairs={{0,16},{16,32},{32,48},{48,64},{64,80},{80,96},{96,112},{112,128},... | collective-permute-start | bytes 49160 | tf_op jit(solution)/shard_map/while/body/eval_jaxpr/ppermute | solution.py:9
  196.3 7.0 %collective-permute-start = (f32[16,256]{1,0:T(8,128)S(1)}, f32[16,256]{1,0:T(8,128)S(1)}, u32[]{:S(2)}, u32[]{:S(2)}) collective-permute-start(f32[16,256]{1,0:T(8,128)S(1)} %get-tuple-element.219), channel_id=1, source_target_pairs={{0,16},{16,32},{32,48},{48,64},{64,80},{80,96},{96,112},{112,128},... | collective-permute-start | bytes 49160 | tf_op jit(solution)/shard_map/while/body/eval_jaxpr/ppermute | solution.py:9
  204.4 6.6 %collective-permute-start = (f32[16,256]{1,0:T(8,128)S(1)}, f32[16,256]{1,0:T(8,128)S(1)}, u32[]{:S(2)}, u32[]{:S(2)}) collective-permute-start(f32[16,256]{1,0:T(8,128)S(1)} %get-tuple-element.219), channel_id=1, source_target_pairs={{0,16},{16,32},{32,48},{48,64},{64,80},{80,96},{96,112},{112,128},... | collective-permute-start | bytes 49160 | tf_op jit(solution)/shard_map/while/body/eval_jaxpr/ppermute | solution.py:9
  212.0 6.6 %collective-permute-start = (f32[16,256]{1,0:T(8,128)S(1)}, f32[16,256]{1,0:T(8,128)S(1)}, u32[]{:S(2)}, u32[]{:S(2)}) collective-permute-start(f32[16,256]{1,0:T(8,128)S(1)} %get-tuple-element.219), channel_id=1, source_target_pairs={{0,16},{16,32},{32,48},{48,64},{64,80},{80,96},{96,112},{112,128},... | collective-permute-start | bytes 49160 | tf_op jit(solution)/shard_map/while/body/eval_jaxpr/ppermute | solution.py:9
  219.5 6.6 %collective-permute-start = (f32[16,256]{1,0:T(8,128)S(1)}, f32[16,256]{1,0:T(8,128)S(1)}, u32[]{:S(2)}, u32[]{:S(2)}) collective-permute-start(f32[16,256]{1,0:T(8,128)S(1)} %get-tuple-element.219), channel_id=1, source_target_pairs={{0,16},{16,32},{32,48},{48,64},{64,80},{80,96},{96,112},{112,128},... | collective-permute-start | bytes 49160 | tf_op jit(solution)/shard_map/while/body/eval_jaxpr/ppermute | solution.py:9
  227.1 6.6 %collective-permute-start = (f32[16,256]{1,0:T(8,128)S(1)}, f32[16,256]{1,0:T(8,128)S(1)}, u32[]{:S(2)}, u32[]{:S(2)}) collective-permute-start(f32[16,256]{1,0:T(8,128)S(1)} %get-tuple-element.219), channel_id=1, source_target_pairs={{0,16},{16,32},{32,48},{48,64},{64,80},{80,96},{96,112},{112,128},... | collective-permute-start | bytes 49160 | tf_op jit(solution)/shard_map/while/body/eval_jaxpr/ppermute | solution.py:9
  234.7 6.6 %collective-permute-start = (f32[16,256]{1,0:T(8,128)S(1)}, f32[16,256]{1,0:T(8,128)S(1)}, u32[]{:S(2)}, u32[]{:S(2)}) collective-permute-start(f32[16,256]{1,0:T(8,128)S(1)} %get-tuple-element.219), channel_id=1, source_target_pairs={{0,16},{16,32},{32,48},{48,64},{64,80},{80,96},{96,112},{112,128},... | collective-permute-start | bytes 49160 | tf_op jit(solution)/shard_map/while/body/eval_jaxpr/ppermute | solution.py:9
  242.3 6.6 %collective-permute-start = (f32[16,256]{1,0:T(8,128)S(1)}, f32[16,256]{1,0:T(8,128)S(1)}, u32[]{:S(2)}, u32[]{:S(2)}) collective-permute-start(f32[16,256]{1,0:T(8,128)S(1)} %get-tuple-element.219), channel_id=1, source_target_pairs={{0,16},{16,32},{32,48},{48,64},{64,80},{80,96},{96,112},{112,128},... | collective-permute-start | bytes 49160 | tf_op jit(solution)/shard_map/while/body/eval_jaxpr/ppermute | solution.py:9
  249.9 6.6 %collective-permute-start = (f32[16,256]{1,0:T(8,128)S(1)}, f32[16,256]{1,0:T(8,128)S(1)}, u32[]{:S(2)}, u32[]{:S(2)}) collective-permute-start(f32[16,256]{1,0:T(8,128)S(1)} %get-tuple-element.219), channel_id=1, source_target_pairs={{0,16},{16,32},{32,48},{48,64},{64,80},{80,96},{96,112},{112,128},... | collective-permute-start | bytes 49160 | tf_op jit(solution)/shard_map/while/body/eval_jaxpr/ppermute | solution.py:9
  257.5 6.6 %collective-permute-start = (f32[16,256]{1,0:T(8,128)S(1)}, f32[16,256]{1,0:T(8,128)S(1)}, u32[]{:S(2)}, u32[]{:S(2)}) collective-permute-start(f32[16,256]{1,0:T(8,128)S(1)} %get-tuple-element.219), channel_id=1, source_target_pairs={{0,16},{16,32},{32,48},{48,64},{64,80},{80,96},{96,112},{112,128},... | collective-permute-start | bytes 49160 | tf_op jit(solution)/shard_map/while/body/eval_jaxpr/ppermute | solution.py:9
  265.1 6.6 %collective-permute-start = (f32[16,256]{1,0:T(8,128)S(1)}, f32[16,256]{1,0:T(8,128)S(1)}, u32[]{:S(2)}, u32[]{:S(2)}) collective-permute-start(f32[16,256]{1,0:T(8,128)S(1)} %get-tuple-element.219), channel_id=1, source_target_pairs={{0,16},{16,32},{32,48},{48,64},{64,80},{80,96},{96,112},{112,128},... | collective-permute-start | bytes 49160 | tf_op jit(solution)/shard_map/while/body/eval_jaxpr/ppermute | solution.py:9
  272.7 6.6 %collective-permute-start = (f32[16,256]{1,0:T(8,128)S(1)}, f32[16,256]{1,0:T(8,128)S(1)}, u32[]{:S(2)}, u32[]{:S(2)}) collective-permute-start(f32[16,256]{1,0:T(8,128)S(1)} %get-tuple-element.219), channel_id=1, source_target_pairs={{0,16},{16,32},{32,48},{48,64},{64,80},{80,96},{96,112},{112,128},... | collective-permute-start | bytes 49160 | tf_op jit(solution)/shard_map/while/body/eval_jaxpr/ppermute | solution.py:9
  280.3 6.6 %collective-permute-start = (f32[16,256]{1,0:T(8,128)S(1)}, f32[16,256]{1,0:T(8,128)S(1)}, u32[]{:S(2)}, u32[]{:S(2)}) collective-permute-start(f32[16,256]{1,0:T(8,128)S(1)} %get-tuple-element.219), channel_id=1, source_target_pairs={{0,16},{16,32},{32,48},{48,64},{64,80},{80,96},{96,112},{112,128},... | collective-permute-start | bytes 49160 | tf_op jit(solution)/shard_map/while/body/eval_jaxpr/ppermute | solution.py:9
  287.9 6.6 %collective-permute-start = (f32[16,256]{1,0:T(8,128)S(1)}, f32[16,256]{1,0:T(8,128)S(1)}, u32[]{:S(2)}, u32[]{:S(2)}) collective-permute-start(f32[16,256]{1,0:T(8,128)S(1)} %get-tuple-element.219), channel_id=1, source_target_pairs={{0,16},{16,32},{32,48},{48,64},{64,80},{80,96},{96,112},{112,128},... | collective-permute-start | bytes 49160 | tf_op jit(solution)/shard_map/while/body/eval_jaxpr/ppermute | solution.py:9
  295.5 6.6 %collective-permute-start = (f32[16,256]{1,0:T(8,128)S(1)}, f32[16,256]{1,0:T(8,128)S(1)}, u32[]{:S(2)}, u32[]{:S(2)}) collective-permute-start(f32[16,256]{1,0:T(8,128)S(1)} %get-tuple-element.219), channel_id=1, source_target_pairs={{0,16},{16,32},{32,48},{48,64},{64,80},{80,96},{96,112},{112,128},... | collective-permute-start | bytes 49160 | tf_op jit(solution)/shard_map/while/body/eval_jaxpr/ppermute | solution.py:9
  303.1 6.6 %collective-permute-start = (f32[16,256]{1,0:T(8,128)S(1)}, f32[16,256]{1,0:T(8,128)S(1)}, u32[]{:S(2)}, u32[]{:S(2)}) collective-permute-start(f32[16,256]{1,0:T(8,128)S(1)} %get-tuple-element.219), channel_id=1, source_target_pairs={{0,16},{16,32},{32,48},{48,64},{64,80},{80,96},{96,112},{112,128},... | collective-permute-start | bytes 49160 | tf_op jit(solution)/shard_map/while/body/eval_jaxpr/ppermute | solution.py:9
  310.7 6.6 %collective-permute-start = (f32[16,256]{1,0:T(8,128)S(1)}, f32[16,256]{1,0:T(8,128)S(1)}, u32[]{:S(2)}, u32[]{:S(2)}) collective-permute-start(f32[16,256]{1,0:T(8,128)S(1)} %get-tuple-element.219), channel_id=1, source_target_pairs={{0,16},{16,32},{32,48},{48,64},{64,80},{80,96},{96,112},{112,128},... | collective-permute-start | bytes 49160 | tf_op jit(solution)/shard_map/while/body/eval_jaxpr/ppermute | solution.py:9
  415.2 16.6 %all-to-all-start.1 = ((f32[16,1,512]{2,1,0:T(1,128)}), f32[16,1,512]{2,1,0:T(1,128)S(1)}, u32[]{:S(2)}, u32[]{:S(2)}) async-start(f32[16,1,512]{2,1,0:T(1,128)} %reshape.352), calls=%async_computation.1 | async-start | bytes 65536 | tf_op jit(solution)/shard_map/all_to_all | solution.py:76
where the time goes:
time: 455 us; the launch traced here: 450 us
  waiting for transfers between devices  155 us (34%)
  blocking collectives  94.9 us (21%)
  starting transfers between devices  79.1 us (17%)
  local copies, waits for them, and re-layouts  43.7 us (10%)
  other arithmetic  41.8 us (9%)
  matrix products  32.5 us (7%)
    ppermute x31, waiting for transfers between devices, passed_along(): lax.ppermute(value, axis, [(i, (i + by) % peers) for i in range(peers)])  148 us
    unnamed x1, blocking collectives  94.9 us
    ppermute x31, starting transfers between devices, passed_along(): lax.ppermute(value, axis, [(i, (i + by) % peers) for i in range(peers)])  59.8 us
    dot_general x32, matrix products, panel_term(): lax.dot_general(panel_now, columns, (((1,), (1,)), ((), ())), precision=l...  31.7 us
    scatter x1, local copies, waits for them, and re-layouts, per_device(): slot_of = jnp.zeros((local_rows,), jnp.int32).at[landing.reshape(-1)].set...  30.4 us
    another operation x2, other arithmetic  18.3 us
    scatter-add x1, other arithmetic, per_device(): correction = jnp.zeros((species, sub_count * cell_count), jnp.float32).at...  14.5 us
    all_to_all x1, starting transfers between devices, per_device(): lax.all_to_all(outgoing, 'sub', split_axis=1, concat_axis=1, tiled=True)  10.1 us
  transfers between devices with their start and end apart: 33, of which 32 were waited for; matrix products, arithmetic and copies ran while one was open for 7% of the time, Pallas kernels for 0%

commit v1 on v0

v1 whole, which is shorter than its diff:
```python
import functools

import jax
import jax.numpy as jnp
from jax import lax
from jax.experimental import pallas as pl
from jax.experimental.pallas import tpu as pltpu
from jax.sharding import Mesh
from jax.sharding import PartitionSpec as P

F32, BF16, I32 = jnp.float32, jnp.bfloat16, jnp.int32
NN = (((1,), (0,)), ((), ()))
NT = (((1,), (1,)), ((), ()))
SUB = ("x", "yh", "c")


def mxu(a, b, dims=NN):
    return lax.dot_general(a, b, dims, preferred_element_type=F32)


def halves(x):
    hi = x.astype(BF16)
    return hi, (x - hi.astype(F32)).astype(BF16)


def thirds(x):
    hi = x.astype(BF16)
    rest = x - hi.astype(F32)
    mid = rest.astype(BF16)
    return hi, mid, (rest - mid.astype(F32)).astype(BF16)


def iota(shape, axis):
    return lax.broadcasted_iota(I32, shape, axis)


def select_rows(x, onehot, dims):
    n = x.shape[0]
    y = mxu(jnp.concatenate(thirds(x), axis=0), onehot, dims)
    return y[:n] + y[n : 2 * n] + y[2 * n :]


def before(n):
    return (iota((n, n), 0) < iota((n, n), 1)).astype(F32).astype(BF16)


def pack(x, store):
    lane = iota((4, 128), 1) // 32
    for u in range(x.shape[1] // 128):
        tile = x[:, u * 128 : (u + 1) * 128]
        turned = [tile] + [pltpu.roll(tile, k * 32, 1) for k in range(1, 4)]
        for v in range(4):
            block = turned[(0 - v) % 4][0:4]
            for b in range(1, 4):
                block = jnp.where(lane == b, turned[(b - v) % 4][4 * b : 4 * b + 4], block)
            store(4 * u + v, block)


def unpack(load, peers):
    lane = iota((4, 128), 1) // 32
    tiles = []
    for u in range(peers // 4):
        blocks = [load(4 * u + v) for v in range(4)]
        turned = [[blk] + [pltpu.roll(blk, k * 32, 1) for k in range(1, 4)] for blk in blocks]
        rows = []
        for b in range(4):
            part = turned[0][(0 - b) % 4]
            for v in range(1, 4):
                part = jnp.where(lane == v, turned[v][(v - b) % 4], part)
            rows.append(part)
        tiles.append(jnp.concatenate(rows, axis=0))
    return jnp.concatenate(tiles, axis=1)


def send_order(map_ref, own, rows, peers, slots):
    target = map_ref[:, pl.ds(pl.multiple_of(own * rows, 128), rows)] // slots
    hit = iota((peers, rows), 0) == target
    ahead = mxu(hit.astype(F32).astype(BF16), before(rows))
    rank = jnp.sum(jnp.where(hit, ahead, 0.0), axis=0, keepdims=True).astype(I32)
    place = target * (rows // peers) + rank
    return (iota((rows, rows), 0) == place).astype(F32).astype(BF16)


def coupling(cells_ref, weights_ref, cells):
    coupled, rows = cells_ref.shape
    cell = iota((cells, rows), 0)
    total = jnp.zeros((cells, rows), F32)
    for c in range(coupled):
        total += jnp.where(cell == cells_ref[c : c + 1, :], weights_ref[c : c + 1, :], 0.0)
    return total


def solve(x, inv_ref, d):
    odd = iota((x.shape[0], 128), 0) % 2 == 1
    return jnp.where(odd, mxu(x, inv_ref[d, 1], NT), mxu(x, inv_ref[d, 0], NT))


def front_kernel(
    own_ref, map_ref, cells_ref, weights_ref, face_ref, rhs_ref, inv_ref, out_ref, sums
):
    subs, twice = rhs_ref.shape[0], rhs_ref.shape[1]
    rows = face_ref.shape[1]
    peers = out_ref.shape[0]
    order = send_order(map_ref, own_ref[0], rows, peers, rows // 2)
    whi, wlo = halves(coupling(cells_ref, weights_ref, 256))
    odd = iota((twice, 128), 0) % 2 == 1
    lane = iota((twice, 128), 1)
    for t in range(subs // 2):
        parts = []
        for d in (2 * t, 2 * t + 1):
            y = solve(rhs_ref[d], inv_ref, d)
            parts.append(
                jnp.concatenate([jnp.where(odd, 0.0, y), jnp.where(odd, y, 0.0)], axis=1)
            )
        hi, lo = halves(jnp.concatenate(parts, axis=0))
        cols = slice(t * 128, (t + 1) * 128)
        z = mxu(jnp.concatenate([hi, lo], axis=0), whi[:, cols])
        z = z[: 2 * twice] + z[2 * twice :] + mxu(hi, wlo[:, cols])
        sums[t] = jnp.where(lane < 64, z[:twice], z[twice:])
    half = twice // 2
    faces = [
        face_ref[:, t * 128 : (t + 1) * 128]
        - (sums[t, pl.ds(0, half, stride=2), :] + sums[t, pl.ds(1, half, stride=2), :])
        for t in range(subs // 2)
    ]
    outgoing = select_rows(jnp.concatenate(faces, axis=1), order, NT)

    def store(t, block):
        out_ref[t] = block

    pack(outgoing, store)


def landing_kernel(own_ref, map_ref, out_ref, targets, slots_of):
    peers = targets.shape[0]
    rows, slots = out_ref.shape
    for p in range(peers):
        targets[p : p + 1, :] = map_ref[:, p * rows : (p + 1) * rows]
    hit = targets[...] // slots == own_ref[0]
    ahead = mxu(hit.astype(F32).astype(BF16), before(rows)).astype(I32)
    key = jnp.where(hit, ahead, -1)
    slot = (targets[...] % slots).astype(F32)
    per = rows // peers
    for p in range(peers):
        mine = iota((per, rows), 0) == key[p : p + 1, :]
        slots_of[p * per : (p + 1) * per, :] = jnp.sum(
            jnp.where(mine, slot[p : p + 1, :], 0.0), axis=1, keepdims=True
        )
    column = slots_of[...].astype(I32)
    out_ref[...] = (iota((rows, slots), 1) == column).astype(F32).astype(BF16)


def assemble_kernel(in_ref, landing_ref, out_ref):
    incoming = unpack(lambda t: in_ref[t], in_ref.shape[0])
    out_ref[...] = select_rows(incoming, landing_ref[...], NN)


def return_kernel(panel_ref, landing_ref, out_ref):
    def store(t, block):
        out_ref[t] = block

    pack(select_rows(panel_ref[...], landing_ref[...], NT), store)


def product_kernel(own_ref, panels_ref, slab_ref, other_ref, out_ref):
    count, species, slots = panels_ref.shape
    rows = slab_ref.shape[0]
    y = own_ref[0]
    total = jnp.zeros((2 * rows, 2 * species), F32)
    low = jnp.zeros((2 * rows, species), F32)
    for z in range(count):
        mine = slab_ref[:, pl.ds(pl.multiple_of((2 * z + y) * slots, 128), slots)]
        both = jnp.concatenate([mine, other_ref[:, z * slots : (z + 1) * slots]], axis=0)
        shi, slo = halves(both)
        phi, plo = halves(panels_ref[z])
        total += mxu(shi, jnp.concatenate([phi, plo], axis=0), NT)
        low += mxu(slo, phi, NT)
    result = total[:, :species] + total[:, species:] + low
    result = jnp.concatenate([result, jnp.zeros((2 * rows, 128 - species), F32)], axis=1)
    out_ref[pl.ds(pl.multiple_of(y * rows, 8), rows), :] = result[:rows]
    out_ref[pl.ds(pl.multiple_of((1 - y) * rows, 8), rows), :] = result[rows:]


def residual_kernel(in_ref, panel_ref, out_ref):
    total = jnp.sum(in_ref[...], axis=0)
    species = panel_ref.shape[0]
    eye = (iota((species, 128), 0) == iota((species, 128), 1)).astype(F32)
    rows = lax.dot_general(eye, total, NT, precision=lax.Precision.HIGHEST, preferred_element_type=F32)
    out_ref[...] = panel_ref[:, : rows.shape[1]] - rows


def back_kernel(
    own_ref, map_ref, cells_ref, weights_ref, in_ref, rhs_ref, inv_ref, out_ref, twofold
):
    subs, twice = rhs_ref.shape[0], rhs_ref.shape[1]
    rows = cells_ref.shape[1]
    peers = in_ref.shape[0]
    order = send_order(map_ref, own_ref[0], rows, peers, rows // 2)
    whi, wlo = halves(coupling(cells_ref, weights_ref, 256))
    values = select_rows(unpack(lambda t: in_ref[t], peers), order, NN)
    half = twice // 2
    for t in range(subs // 2):
        twofold[t, pl.ds(0, half, stride=2), :] = values[:, t * 128 : (t + 1) * 128]
        twofold[t, pl.ds(1, half, stride=2), :] = values[:, t * 128 : (t + 1) * 128]
    odd = iota((twice, 128), 0) % 2 == 1
    lane = iota((twice, 128), 1)
    for t in range(subs // 2):
        cols = slice(t * 128, (t + 1) * 128)
        v = twofold[t]
        hi, lo = halves(jnp.concatenate([jnp.where(lane < 64, v, 0.0), jnp.where(lane < 64, 0.0, v)], axis=0))
        z = mxu(jnp.concatenate([hi, lo], axis=0), whi[:, cols], NT)
        z = z[: 2 * twice] + z[2 * twice :] + mxu(hi, wlo[:, cols], NT)
        for i, d in enumerate((2 * t, 2 * t + 1)):
            part = z[i * twice : (i + 1) * twice]
            correction = jnp.where(odd, part[:, 128:], part[:, :128])
            reduced = (rhs_ref[d].astype(F32) - correction).astype(BF16)
            out_ref[d] = solve(reduced, inv_ref, d)


SMEM = pl.BlockSpec(memory_space=pltpu.SMEM)
VMEM = pl.BlockSpec(memory_space=pltpu.VMEM)


def call(kernel, name, shape, *args, dtype=F32, scratch=()):
    specs = [SMEM if a.ndim == 1 else VMEM for a in args]
    return pl.pallas_call(
        kernel,
        out_shape=jax.ShapeDtypeStruct(shape, dtype),
        in_specs=specs,
        out_specs=VMEM,
        scratch_shapes=scratch,
        name=name,
    )(*args)


def per_device(rhs, inverse, rhs_face, cells, weights, group_map, slab):
    subs, species, blocks, width = rhs.shape
    rows = rhs_face.shape[1]
    slots = rows // 2
    peers = lax.axis_size(SUB)
    levels = lax.axis_size("z")
    slab_rows = slab.shape[0]
    own = lax.axis_index(SUB).astype(I32).reshape(1)
    side = lax.axis_index("yl").astype(I32).reshape(1)
    rhs2 = rhs.reshape(subs, species * blocks, width)

    outgoing = call(
        front_kernel, "front", (peers, 4, 128), own, group_map, cells, weights, rhs_face, rhs2,
        inverse, scratch=[pltpu.VMEM((subs // 2, species * blocks, 128), F32)],
    )
    incoming = lax.all_to_all(outgoing, SUB, 0, 0)
    paired = slab.reshape(slab_rows, levels, 2, slots)
    away = jnp.where(side[0] == 0, paired[:, :, 1], paired[:, :, 0]).reshape(slab_rows, levels * slots)
    other = lax.ppermute(away, "yl", [(0, 1), (1, 0)])
    landing = call(
        landing_kernel, "landing", (rows, slots), own, group_map, dtype=BF16,
        scratch=[pltpu.VMEM((peers, rows), I32), pltpu.VMEM((rows, 1), F32)],
    )
    panel = call(assemble_kernel, "assemble", (species, slots), incoming, landing)
    panels = lax.all_to_all(jnp.broadcast_to(panel[None], (levels, species, slots)), "z", 0, 0)
    returning = call(return_kernel, "giveback", (peers, 4, 128), panel, landing)
    returned = lax.all_to_all(returning, SUB, 0, 0)
    update = call(
        back_kernel, "back", (subs, species * blocks, width), own, group_map, cells, weights,
        returned, rhs2, inverse, scratch=[pltpu.VMEM((subs // 2, species * blocks, 128), F32)],
    )
    partial = call(product_kernel, "product", (2 * slab_rows, 128), side, panels, slab, other)
    partial = partial.reshape(2 * peers, slab_rows // peers, 128)
    shares = lax.all_to_all(partial, ("yl",) + SUB, 0, 0)
    residual = call(residual_kernel, "residual", (species, slab_rows // peers), shares, panel)
    return update.reshape(rhs.shape), residual


def solution(mesh):
    fine = Mesh(mesh.devices.reshape(16, 2, 4, 2, 2), ("z", "yl", "x", "yh", "c"))
    blk, sub = ("z", "yl"), SUB
    every = blk + sub
    placed = (
        P(every, None, None, None),
        P(every, None, None, None),
        P(None, every),
        P(None, every),
        P(None, every),
        P(blk, None),
        P(blk, sub),
    )
    return jax.shard_map(
        per_device,
        mesh=fine,
        in_specs=placed,
        out_specs=(P(every, None, None, None), P(None, every)),
        check_vma=False,
    )
```

time: 455 us -> 105 us (0.23); the launches traced: 450 us -> 105 us
  waiting for transfers between devices: 155 us -> 32.8 us
  blocking collectives: 94.9 us -> 0 us
  other arithmetic: 41.8 us -> 1.43 us
  starting transfers between devices: 79.1 us -> 40.9 us
  matrix products: 32.5 us -> 0 us
  local copies, waits for them, and re-layouts: 43.7 us -> 12 us
  Pallas kernels: 0 us -> 16.8 us
    ppermute x31 -> x1, waiting for transfers between devices: 148 us -> 0.01 us  [per_device(): other = lax.ppermute(away, 'yl', [(0, 1), (1, 0)])]
    unnamed x1 -> x0, blocking collectives: 94.9 us -> none
    ppermute x31 -> x1, starting transfers between devices: 59.8 us -> 4.02 us  [per_device(): other = lax.ppermute(away, 'yl', [(0, 1), (1, 0)])]
    dot_general x34 -> x0, matrix products: 32.5 us -> none  [the longest x32 31.7 us: panel_term(): lax.dot_general(panel_now, columns, (((1,), (1,)), ((), ())), precision=l...]
    scatter x1 -> x0, local copies, waits for them, and re-layouts: 30.4 us -> none  [per_device(): slot_of = jnp.zeros((local_rows,), jnp.int32).at[landing.reshape(-1)].set...]
    all_to_all x2 -> x4, waiting for transfers between devices: 6.8 us -> 32.8 us  [the longest x1 13.7 us: per_device(): incoming = lax.all_to_all(outgoing, SUB, 0, 0)]
    another operation x2 -> x0, other arithmetic: 18.3 us -> none
    all_to_all x2 -> x4, starting transfers between devices: 19.4 us -> 36.9 us  [the longest x1 14.9 us: per_device(): lax.all_to_all(jnp.broadcast_to(panel[None], (levels, species, slots)), '...]
  transfers between devices with their start and end apart: 33 -> 5, of which waited for: 32 -> 4; matrix products, arithmetic and copies ran while one was open for 7% -> 1% of each run, Pallas kernels for 0% -> 15%
where the time goes in v1:
time: 105 us
  starting transfers between devices  40.9 us (39%)
  waiting for transfers between devices  32.8 us (31%)
  Pallas kernels  16.8 us (16%)
  local copies, waits for them, and re-layouts  12 us (11%)
  other arithmetic  1.43 us (1%)
    pallas_call x7, Pallas kernels, call(): pl.pallas_call(kernel, out_shape=jax.ShapeDtypeStruct(shape, dtype), in_s...  16.8 us
    all_to_all x1, starting transfers between devices, per_device(): lax.all_to_all(jnp.broadcast_to(panel[None], (levels, species, slots)), '...  14.9 us
    all_to_all x1, waiting for transfers between devices, per_device(): incoming = lax.all_to_all(outgoing, SUB, 0, 0)  13.7 us
    all_to_all x1, waiting for transfers between devices, per_device(): lax.all_to_all(jnp.broadcast_to(panel[None], (levels, species, slots)), '...  12.1 us
    all_to_all x1, starting transfers between devices, per_device(): returned = lax.all_to_all(returning, SUB, 0, 0)  9.59 us
    all_to_all x1, starting transfers between devices, per_device(): incoming = lax.all_to_all(outgoing, SUB, 0, 0)  8.02 us
    all_to_all x1, starting transfers between devices, per_device(): shares = lax.all_to_all(partial, ('yl',) + SUB, 0, 0)  4.35 us
    unnamed x12, local copies, waits for them, and re-layouts  4.16 us
  transfers between devices with their start and end apart: 5, of which 4 were waited for; matrix products, arithmetic and copies ran while one was open for 1% of the time, Pallas kernels for 15%

profile of v1, /device:TPU:1, one launch (start us, length us, event | category | flops | bytes accessed | tf_op | source)
XLA Modules:
  0.0 104.7 jit_solution(4098194763453938892)
XLA Ops:
  0.6 3.0 %reshape.32 = f32[64,16,2,256]{3,2,1,0:T(2,128)S(1)} reshape(f32[64,8192]{1,0:T(8,128)} %slab_ref.1) | data formatting | bytes 4194304 | tf_op jit(solution)/shard_map/reshape | solution.py:252
  3.7 3.4 %fusion = (f32[64,16,1,256]{3,2,1,0:T(1,128)S(1)}, f32[64,16,1,256]{3,2,1,0:T(1,128)}) fusion(f32[64,16,2,256]{3,2,1,0:T(2,128)S(1)} %reshape.32), kind=kLoop, calls=%fused_computation.1 | loop fusion | bytes 4194304 | tf_op jit(solution)/shard_map/slice | solution.py:253
  7.0 1.4 %copy_select_fusion = f32[64,16,1,256]{3,1,0,2:T(8,128)S(1)} fusion(f32[64,16,1,256]{3,2,1,0:T(1,128)} %get-tuple-element.5, f32[64,16,1,256]{3,2,1,0:T(1,128)S(1)} %get-tuple-element.4, pred[]{:T(512)S(6)} %eq.3), kind=kLoop, calls=%fused_computation | loop fusion | flops 262144 | bytes 3145729 | tf_op jit(solution)/shard_map/jit(_where)/select_n | solution.py:253
  8.5 0.6 copy.14
  9.1 4.0 %collective-permute-start = (f32[64,4096]{1,0:T(8,128)S(1)}, f32[64,4096]{1,0:T(8,128)S(1)}, u32[]{:S(2)}, u32[]{:S(2)}) collective-permute-start(f32[64,4096]{1,0:T(8,128)S(1)} %bitcast.10), channel_id=1, source_target_pairs={{0,16},{16,0},{1,17},{17,1},{2,18},{18,2},{3,19},{19,3},{4,20},{20... | collective-permute-start | bytes 3145736 | tf_op jit(solution)/shard_map/ppermute | solution.py:254
  13.1 3.0 %front.1 = f32[16,4,128]{2,1,0:T(4,128)} custom-call(s32[1]{0:T(128)} %bitcast.own_ref, s32[1,8192]{1,0:T(1,128)} %map_ref.5, s32[5,512]{1,0:T(8,128)} %cells_ref.3, f32[5,512]{1,0:T(8,128)} %weights_ref.3, f32[16,512]{1,0:T(8,128)} %face_ref.1, bf16[8,32,128]{2,1,0:T(8,128)(2,1)} %bitcast.12, bf16[8,2,128,128]{3,2,1,0:T(8,128)(2,1)} %inv_ref.3), custom_call_target="tpu_custom_call" | custom-call | tf_op jit(solution)/shard_map/front/pallas_call | solution.py:226
  16.1 8.0 %all-to-all-start = ((f32[16,4,128]{2,1,0:T(4,128)}), f32[16,4,128]{2,1,0:T(4,128)S(1)}, u32[]{:S(2)}, u32[]{:S(2)}) async-start(f32[16,4,128]{2,1,0:T(4,128)} %front.1), calls=%async_computation | async-start | bytes 65536 | tf_op jit(solution)/shard_map/all_to_all | solution.py:251
  24.2 1.9 %landing.1.landing_ref = bf16[512,256]{1,0:T(8,128)(2,1)} custom-call(s32[1]{0:T(128)} %bitcast.own_ref, s32[1,8192]{1,0:T(1,128)} %map_ref.5), custom_call_target="tpu_custom_call" | custom-call | tf_op jit(solution)/shard_map/landing/pallas_call | solution.py:226
  26.1 13.7 %all-to-all-done.in_ref = f32[16,4,128]{2,1,0:T(4,128)S(1)} async-done(((f32[16,4,128]{2,1,0:T(4,128)}), f32[16,4,128]{2,1,0:T(4,128)S(1)}, u32[]{:S(2)}, u32[]{:S(2)}) %all-to-all-start) | async-done | bytes 32800 | tf_op jit(solution)/shard_map/all_to_all | solution.py:251
  39.8 0.0 copy-start.4
  39.8 0.6 copy-done.4
  40.4 1.8 %assemble.1.panel_ref = f32[16,256]{1,0:T(8,128)} custom-call(f32[16,4,128]{2,1,0:T(4,128)} %copy-done.4, bf16[512,256]{1,0:T(8,128)(2,1)} %landing.1.landing_ref), custom_call_target="tpu_custom_call" | custom-call | tf_op jit(solution)/shard_map/assemble/pallas_call | solution.py:226
  42.2 1.4 %broadcast_in_dim.2 = f32[16,16,256]{2,1,0:T(8,128)} broadcast(f32[16,256]{1,0:T(8,128)} %assemble.1.panel_ref), dimensions={1,2} | broadcast | bytes 278528 | tf_op jit(solution)/shard_map/broadcast_in_dim | solution.py:260
  43.7 14.9 %all-to-all-start.2 = ((f32[16,16,256]{2,1,0:T(8,128)}), f32[16,16,256]{2,1,0:T(8,128)S(1)}, u32[]{:S(2)}, u32[]{:S(2)}) async-start(f32[16,16,256]{2,1,0:T(8,128)} %broadcast_in_dim.2), calls=%async_computation.2 | async-start | bytes 524288 | tf_op jit(solution)/shard_map/all_to_all | solution.py:260
  58.6 1.9 %giveback.1 = f32[16,4,128]{2,1,0:T(4,128)} custom-call(f32[16,256]{1,0:T(8,128)} %assemble.1.panel_ref, bf16[512,256]{1,0:T(8,128)(2,1)} %landing.1.landing_ref), custom_call_target="tpu_custom_call" | custom-call | tf_op jit(solution)/shard_map/giveback/pallas_call | solution.py:226
  60.5 12.1 %all-to-all-done.2.panels_ref = f32[16,16,256]{2,1,0:T(8,128)S(1)} async-done(((f32[16,16,256]{2,1,0:T(8,128)}), f32[16,16,256]{2,1,0:T(8,128)S(1)}, u32[]{:S(2)}, u32[]{:S(2)}) %all-to-all-start.2) | async-done | bytes 262176 | tf_op jit(solution)/shard_map/all_to_all | solution.py:260
  72.6 0.0 copy-start
  72.6 9.6 %all-to-all-start.1 = ((f32[16,4,128]{2,1,0:T(4,128)}), f32[16,4,128]{2,1,0:T(4,128)S(1)}, u32[]{:S(2)}, u32[]{:S(2)}) async-start(f32[16,4,128]{2,1,0:T(4,128)} %giveback.1), calls=%async_computation.1 | async-start | bytes 65536 | tf_op jit(solution)/shard_map/all_to_all | solution.py:262
  82.2 0.0 collective-permute-done.other_ref
  82.2 0.0 copy-start.1
  82.2 0.0 copy-done
  82.2 1.0 copy-done.1
  83.2 3.3 %product.1 = f32[128,128]{1,0:T(8,128)} custom-call(s32[1]{0:T(128)} %bitcast.3.own_ref, f32[16,16,256]{2,1,0:T(8,128)} %copy-done, f32[64,8192]{1,0:T(8,128)} %slab_ref.1, f32[64,4096]{1,0:T(8,128)} %copy-done.1), custom_call_target="tpu_custom_call" | custom-call | tf_op jit(solution)/shard_map/product/pallas_call | solution.py:226
  86.5 3.0 %all-to-all-done.1.in_ref = f32[16,4,128]{2,1,0:T(4,128)S(1)} async-done(((f32[16,4,128]{2,1,0:T(4,128)}), f32[16,4,128]{2,1,0:T(4,128)S(1)}, u32[]{:S(2)}, u32[]{:S(2)}) %all-to-all-start.1) | async-done | bytes 32800 | tf_op jit(solution)/shard_map/all_to_all | solution.py:262
  89.5 0.0 copy-start.3
  89.5 4.3 %all-to-all-start.3 = ((f32[32,4,128]{2,1,0:T(4,128)}), f32[32,4,128]{2,1,0:T(4,128)S(1)}, u32[]{:S(2)}, u32[]{:S(2)}) async-start(f32[32,4,128]{2,1,0:T(4,128)} %bitcast.11), calls=%async_computation.3 | async-start | bytes 131072 | tf_op jit(solution)/shard_map/all_to_all | solution.py:269
  93.8 0.0 copy-done.3
  93.9 3.2 %back.1 = f32[8,32,128]{2,1,0:T(8,128)} custom-call(s32[1]{0:T(128)} %bitcast.own_ref, s32[1,8192]{1,0:T(1,128)} %map_ref.5, s32[5,512]{1,0:T(8,128)} %cells_ref.3, f32[5,512]{1,0:T(8,128)} %weights_ref.3, f32[16,4,128]{2,1,0:T(4,128)} %copy-done.3, bf16[8,32,128]{2,1,0:T(8,128)(2,1)} %bitcast.13, bf16[8,2,128,128]{3,2,1,0:T(8,128)(2,1)} %inv_ref.3), custom_call_target="tpu_custom_call" | custom-call | tf_op jit(solution)/shard_map/back/pallas_call | solution.py:226
  97.1 4.0 %all-to-all-done.3.in_ref = f32[32,4,128]{2,1,0:T(4,128)S(1)} async-done(((f32[32,4,128]{2,1,0:T(4,128)}), f32[32,4,128]{2,1,0:T(4,128)S(1)}, u32[]{:S(2)}, u32[]{:S(2)}) %all-to-all-start.3) | async-done | bytes 65568 | tf_op jit(solution)/shard_map/all_to_all | solution.py:269
  101.1 0.0 copy-start.2
  101.1 0.6 copy-done.2
  101.8 1.6 %residual.1 = f32[16,4]{1,0:T(8,128)} custom-call(f32[32,4,128]{2,1,0:T(4,128)} %copy-done.2, f32[16,256]{1,0:T(8,128)} %assemble.1.panel_ref), custom_call_target="tpu_custom_call" | custom-call | tf_op jit(solution)/shard_map/residual/pallas_call | solution.py:226
  103.3 1.3 %copy.11 = f32[16,4]{0,1:T(4,128)} copy(f32[16,4]{1,0:T(8,128)} %residual.1) | data formatting | bytes 512
Async XLA Ops:
  9.1 73.1 %collective-permute-start = (f32[64,4096]{1,0:T(8,128)S(1)}, f32[64,4096]{1,0:T(8,128)S(1)}, u32[]{:S(2)}, u32[]{:S(2)}) collective-permute-start(f32[64,4096]{1,0:T(8,128)S(1)} %bitcast.10), channel_id=1, source_target_pairs={{0,16},{16,0},{1,17},{17,1},{2,18},{18,2},{3,19},{19,3},{4,20},{20... | collective-permute-start | bytes 3145736 | tf_op jit(solution)/shard_map/ppermute | solution.py:254
  16.1 23.6 %all-to-all-start = ((f32[16,4,128]{2,1,0:T(4,128)}), f32[16,4,128]{2,1,0:T(4,128)S(1)}, u32[]{:S(2)}, u32[]{:S(2)}) async-start(f32[16,4,128]{2,1,0:T(4,128)} %front.1), calls=%async_computation | async-start | bytes 65536 | tf_op jit(solution)/shard_map/all_to_all | solution.py:251
  39.8 0.6 copy-start.4
  43.7 28.9 %all-to-all-start.2 = ((f32[16,16,256]{2,1,0:T(8,128)}), f32[16,16,256]{2,1,0:T(8,128)S(1)}, u32[]{:S(2)}, u32[]{:S(2)}) async-start(f32[16,16,256]{2,1,0:T(8,128)} %broadcast_in_dim.2), calls=%async_computation.2 | async-start | bytes 524288 | tf_op jit(solution)/shard_map/all_to_all | solution.py:260
  72.6 9.6 %copy-start = (f32[16,16,256]{2,1,0:T(8,128)}, f32[16,16,256]{2,1,0:T(8,128)S(1)}, u32[]{:S(2)}) copy-start(f32[16,16,256]{2,1,0:T(8,128)S(1)} %all-to-all-done.2.panels_ref) | copy-start | bytes 786436
  72.6 16.9 %all-to-all-start.1 = ((f32[16,4,128]{2,1,0:T(4,128)}), f32[16,4,128]{2,1,0:T(4,128)S(1)}, u32[]{:S(2)}, u32[]{:S(2)}) async-start(f32[16,4,128]{2,1,0:T(4,128)} %giveback.1), calls=%async_computation.1 | async-start | bytes 65536 | tf_op jit(solution)/shard_map/all_to_all | solution.py:262
  82.2 1.0 copy-start.1
  89.5 4.4 %copy-start.3 = (f32[16,4,128]{2,1,0:T(4,128)}, f32[16,4,128]{2,1,0:T(4,128)S(1)}, u32[]{:S(2)}) copy-start(f32[16,4,128]{2,1,0:T(4,128)S(1)} %all-to-all-done.1.in_ref) | copy-start | bytes 98308
  89.5 11.6 %all-to-all-start.3 = ((f32[32,4,128]{2,1,0:T(4,128)}), f32[32,4,128]{2,1,0:T(4,128)S(1)}, u32[]{:S(2)}, u32[]{:S(2)}) async-start(f32[32,4,128]{2,1,0:T(4,128)} %bitcast.11), calls=%async_computation.3 | async-start | bytes 131072 | tf_op jit(solution)/shard_map/all_to_all | solution.py:269
  101.1 0.6 copy-start.2

commit v2 on v1

--- a/solution.py
+++ b/solution.py
@@ -72,8 +72,9 @@
     return jnp.concatenate(tiles, axis=1)
 
 
-def send_order(map_ref, own, rows, peers, slots):
-    target = map_ref[:, pl.ds(pl.multiple_of(own * rows, 128), rows)] // slots
+def send_order(mapped, peers, slots):
+    rows = mapped.shape[1]
+    target = mapped // slots
     hit = iota((peers, rows), 0) == target
     ahead = mxu(hit.astype(F32).astype(BF16), before(rows))
     rank = jnp.sum(jnp.where(hit, ahead, 0.0), axis=0, keepdims=True).astype(I32)
@@ -96,13 +97,36 @@
 
 
 def front_kernel(
-    own_ref, map_ref, cells_ref, weights_ref, face_ref, rhs_ref, inv_ref, out_ref, sums
+    own_ref, map_hbm, cells_hbm, weights_hbm, face_hbm, rhs_hbm, inv_hbm,
+    out_ref, order_ref, whi_ref, wlo_ref,
+    sums, map_ref, cells_ref, weights_ref, face_ref, rhs_ref, inv_ref, sems,
 ):
     subs, twice = rhs_ref.shape[0], rhs_ref.shape[1]
     rows = face_ref.shape[1]
     peers = out_ref.shape[0]
-    order = send_order(map_ref, own_ref[0], rows, peers, rows // 2)
-    whi, wlo = halves(coupling(cells_ref, weights_ref, 256))
+    here = pl.ds(pl.multiple_of(own_ref[0] * rows, 128), rows)
+    copies = [
+        pltpu.make_async_copy(source, target, sems.at[i])
+        for i, (source, target) in enumerate(
+            (
+                (map_hbm.at[:, here], map_ref),
+                (cells_hbm, cells_ref),
+                (weights_hbm, weights_ref),
+                (face_hbm, face_ref),
+                (rhs_hbm, rhs_ref),
+                (inv_hbm, inv_ref),
+            )
+        )
+    ]
+    for copy in copies:
+        copy.start()
+    for copy in copies[:3]:
+        copy.wait()
+    order = send_order(map_ref[...], peers, rows // 2)
+    whi, wlo = halves(coupling(cells_ref, weights_ref, whi_ref.shape[0]))
+    order_ref[...], whi_ref[...], wlo_ref[...] = order, whi, wlo
+    for copy in copies[3:]:
+        copy.wait()
     odd = iota((twice, 128), 0) % 2 == 1
     lane = iota((twice, 128), 1)
     for t in range(subs // 2):
@@ -150,54 +174,86 @@
     out_ref[...] = (iota((rows, slots), 1) == column).astype(F32).astype(BF16)
 
 
+def column_of(j, side):
+    if POOL == "yl":
+        return 2 * j + side
+    return 4 * (j // 2) + 2 * side + j % 2
+
+
+def cut_kernel(side_ref, slab_ref, away_ref, hi_ref, lo_ref, mine, sems):
+    slots = SLOTS
+    count = away_ref.shape[1] // slots
+    side = side_ref[0]
+    copies = []
+    for j in range(count):
+        here = pl.ds(j * slots, slots)
+        for i, (member, target) in enumerate(((1 - side, away_ref), (side, mine))):
+            there = pl.ds(pl.multiple_of(column_of(j, member) * slots, 128), slots)
+            copy = pltpu.make_async_copy(
+                slab_ref.at[:, there], target.at[:, here], sems.at[i, j]
+            )
+            copy.start()
+            copies.append(copy)
+    for copy in copies:
+        copy.wait()
+    hi, lo = halves(mine[...])
+    hi_ref[...], lo_ref[...] = hi, lo
+
+
 def assemble_kernel(in_ref, landing_ref, out_ref):
     incoming = unpack(lambda t: in_ref[t], in_ref.shape[0])
     out_ref[...] = select_rows(incoming, landing_ref[...], NN)
 
 
-def return_kernel(panel_ref, landing_ref, out_ref):
-    def store(t, block):
-        out_ref[t] = block
-
-    pack(select_rows(panel_ref[...], landing_ref[...], NT), store)
-
-
-def product_kernel(own_ref, panels_ref, slab_ref, other_ref, out_ref):
+def product_kernel(
+    side_ref, panels_ref, hi_ref, lo_ref, other_ref, panel_ref, landing_ref, out_ref
+):
     count, species, slots = panels_ref.shape
-    rows = slab_ref.shape[0]
-    y = own_ref[0]
+    rows = hi_ref.shape[0]
+    peers = out_ref.shape[0] // 2
+    side = side_ref[0]
     total = jnp.zeros((2 * rows, 2 * species), F32)
     low = jnp.zeros((2 * rows, species), F32)
-    for z in range(count):
-        mine = slab_ref[:, pl.ds(pl.multiple_of((2 * z + y) * slots, 128), slots)]
-        both = jnp.concatenate([mine, other_ref[:, z * slots : (z + 1) * slots]], axis=0)
-        shi, slo = halves(both)
-        phi, plo = halves(panels_ref[z])
+    for j in range(count):
+        cols = slice(j * slots, (j + 1) * slots)
+        ohi, olo = halves(other_ref[:, cols])
+        phi, plo = halves(panels_ref[j])
+        shi = jnp.concatenate([hi_ref[:, cols], ohi], axis=0)
+        slo = jnp.concatenate([lo_ref[:, cols], olo], axis=0)
         total += mxu(shi, jnp.concatenate([phi, plo], axis=0), NT)
         low += mxu(slo, phi, NT)
     result = total[:, :species] + total[:, species:] + low
     result = jnp.concatenate([result, jnp.zeros((2 * rows, 128 - species), F32)], axis=1)
-    out_ref[pl.ds(pl.multiple_of(y * rows, 8), rows), :] = result[:rows]
-    out_ref[pl.ds(pl.multiple_of((1 - y) * rows, 8), rows), :] = result[rows:]
-
-
-def residual_kernel(in_ref, panel_ref, out_ref):
-    total = jnp.sum(in_ref[...], axis=0)
-    species = panel_ref.shape[0]
-    eye = (iota((species, 128), 0) == iota((species, 128), 1)).astype(F32)
-    rows = lax.dot_general(eye, total, NT, precision=lax.Precision.HIGHEST, preferred_element_type=F32)
-    out_ref[...] = panel_ref[:, : rows.shape[1]] - rows
+    mine, other = side * peers, (1 - side) * peers
+    per = rows // peers
+    nothing = jnp.zeros((4, 128), F32)
+    for p in range(peers):
+        out_ref[mine + p, 0:per, :] = result[p * per : (p + 1) * per]
+        out_ref[other + p, 0:per, :] = result[rows + p * per : rows + (p + 1) * per]
+        out_ref[other + p, per : per + 4, :] = nothing
+
+    def store(t, block):
+        out_ref[mine + t, per : per + 4, :] = block
+
+    pack(select_rows(panel_ref[...], landing_ref[...], NT), store)
 
 
 def back_kernel(
-    own_ref, map_ref, cells_ref, weights_ref, in_ref, rhs_ref, inv_ref, out_ref, twofold
+    side_ref, in_ref, panel_ref, order_ref, whi_ref, wlo_ref, rhs_ref, inv_ref,
+    out_ref, residual_ref, twofold,
 ):
     subs, twice = rhs_ref.shape[0], rhs_ref.shape[1]
-    rows = cells_ref.shape[1]
-    peers = in_ref.shape[0]
-    order = send_order(map_ref, own_ref[0], rows, peers, rows // 2)
-    whi, wlo = halves(coupling(cells_ref, weights_ref, 256))
-    values = select_rows(unpack(lambda t: in_ref[t], peers), order, NN)
+    peers = in_ref.shape[0] // 2
+    per, species = residual_ref.shape
+    total = jnp.sum(in_ref[...], axis=0)
+    eye = (iota((8, 128), 0) == iota((8, 128), 1)).astype(F32)
+    first = lax.dot_general(
+        eye, panel_ref[:, :128], NT, precision=lax.Precision.HIGHEST, preferred_element_type=F32
+    )
+    residual_ref[...] = (first - total[:, :species])[:per]
+    mine = side_ref[0] * peers
+    returned = unpack(lambda t: in_ref[mine + t, per : per + 4, :], peers)
+    values = select_rows(returned, order_ref[...], NN)
     half = twice // 2
     for t in range(subs // 2):
         twofold[t, pl.ds(0, half, stride=2), :] = values[:, t * 128 : (t + 1) * 128]
@@ -207,9 +263,11 @@
     for t in range(subs // 2):
         cols = slice(t * 128, (t + 1) * 128)
         v = twofold[t]
-        hi, lo = halves(jnp.concatenate([jnp.where(lane < 64, v, 0.0), jnp.where(lane < 64, 0.0, v)], axis=0))
-        z = mxu(jnp.concatenate([hi, lo], axis=0), whi[:, cols], NT)
-        z = z[: 2 * twice] + z[2 * twice :] + mxu(hi, wlo[:, cols], NT)
+        hi, lo = halves(
+            jnp.concatenate([jnp.where(lane < 64, v, 0.0), jnp.where(lane < 64, 0.0, v)], axis=0)
+        )
+        z = mxu(jnp.concatenate([hi, lo], axis=0), whi_ref[:, cols], NT)
+        z = z[: 2 * twice] + z[2 * twice :] + mxu(hi, wlo_ref[:, cols], NT)
         for i, d in enumerate((2 * t, 2 * t + 1)):
             part = z[i * twice : (i + 1) * twice]
             correction = jnp.where(odd, part[:, 128:], part[:, :128])
@@ -217,19 +275,37 @@
             out_ref[d] = solve(reduced, inv_ref, d)
 
 
-SMEM = pl.BlockSpec(memory_space=pltpu.SMEM)
-VMEM = pl.BlockSpec(memory_space=pltpu.VMEM)
-
-
-def call(kernel, name, shape, *args, dtype=F32, scratch=()):
-    specs = [SMEM if a.ndim == 1 else VMEM for a in args]
+POOL = "yl"
+GATHER = ("zh", "zl") if POOL == "yl" else ("zh", "yl")
+RING = False
+SLOTS = 256
+VMEM = pltpu.VMEM
+
+
+def vm(x):
+    return pltpu.with_memory_space_constraint(x, pltpu.VMEM)
+
+
+def call(kernel, name, outs, *args, scratch=(), hbm=()):
+    specs = [
+        pl.BlockSpec(
+            memory_space=pltpu.SMEM if a.ndim == 1 else pltpu.HBM if i in hbm else pltpu.VMEM
+        )
+        for i, a in enumerate(args)
+    ]
+    args = [
+        pltpu.with_memory_space_constraint(a, pltpu.HBM) if i in hbm else a
+        for i, a in enumerate(args)
+    ]
+    whole = pl.BlockSpec(memory_space=pltpu.VMEM)
     return pl.pallas_call(
         kernel,
-        out_shape=jax.ShapeDtypeStruct(shape, dtype),
+        out_shape=outs,
         in_specs=specs,
-        out_specs=VMEM,
+        out_specs=[whole] * len(outs) if isinstance(outs, list) else whole,
         scratch_shapes=scratch,
         name=name,
+        compiler_params=pltpu.CompilerParams(vmem_limit_bytes=16 << 20),
     )(*args)
 
 
@@ -238,42 +314,83 @@
     rows = rhs_face.shape[1]
     slots = rows // 2
     peers = lax.axis_size(SUB)
-    levels = lax.axis_size("z")
+    levels = lax.axis_size(GATHER)
     slab_rows = slab.shape[0]
     own = lax.axis_index(SUB).astype(I32).reshape(1)
-    side = lax.axis_index("yl").astype(I32).reshape(1)
+    side = lax.axis_index(POOL).astype(I32).reshape(1)
     rhs2 = rhs.reshape(subs, species * blocks, width)
-
-    outgoing = call(
-        front_kernel, "front", (peers, 4, 128), own, group_map, cells, weights, rhs_face, rhs2,
-        inverse, scratch=[pltpu.VMEM((subs // 2, species * blocks, 128), F32)],
+    pairs = VMEM((subs // 2, species * blocks, 128), F32)
+
+    outgoing, order, whi, wlo = call(
+        front_kernel,
+        "front",
+        [
+            VMEM((peers, 4, 128), F32),
+            VMEM((rows, rows), BF16),
+            VMEM((blocks * width, rows), BF16),
+            VMEM((blocks * width, rows), BF16),
+        ],
+        own, group_map, cells, weights, rhs_face, rhs2, inverse,
+        scratch=[pairs]
+        + [
+            VMEM(shape, kind)
+            for shape, kind in (
+                ((1, rows), I32),
+                (cells.shape, I32),
+                (weights.shape, F32),
+                (rhs_face.shape, F32),
+                (rhs2.shape, BF16),
+                (inverse.shape, BF16),
+            )
+        ]
+        + [pltpu.SemaphoreType.DMA((6,))],
+        hbm=range(1, 7),
     )
     incoming = lax.all_to_all(outgoing, SUB, 0, 0)
-    paired = slab.reshape(slab_rows, levels, 2, slots)
-    away = jnp.where(side[0] == 0, paired[:, :, 1], paired[:, :, 0]).reshape(slab_rows, levels * slots)
-    other = lax.ppermute(away, "yl", [(0, 1), (1, 0)])
+    half = levels * slots
+    away, hi, lo = call(
+        cut_kernel,
+        "cut",
+        [VMEM((slab_rows, half), F32), VMEM((slab_rows, half), BF16), VMEM((slab_rows, half), BF16)],
+        side, slab,
+        scratch=[VMEM((slab_rows, half), F32), pltpu.SemaphoreType.DMA((2, levels))],
+        hbm=(1,),
+    )
     landing = call(
-        landing_kernel, "landing", (rows, slots), own, group_map, dtype=BF16,
-        scratch=[pltpu.VMEM((peers, rows), I32), pltpu.VMEM((rows, 1), F32)],
-    )
-    panel = call(assemble_kernel, "assemble", (species, slots), incoming, landing)
-    panels = lax.all_to_all(jnp.broadcast_to(panel[None], (levels, species, slots)), "z", 0, 0)
-    returning = call(return_kernel, "giveback", (peers, 4, 128), panel, landing)
-    returned = lax.all_to_all(returning, SUB, 0, 0)
-    update = call(
-        back_kernel, "back", (subs, species * blocks, width), own, group_map, cells, weights,
-        returned, rhs2, inverse, scratch=[pltpu.VMEM((subs // 2, species * blocks, 128), F32)],
-    )
-    partial = call(product_kernel, "product", (2 * slab_rows, 128), side, panels, slab, other)
-    partial = partial.reshape(2 * peers, slab_rows // peers, 128)
-    shares = lax.all_to_all(partial, ("yl",) + SUB, 0, 0)
-    residual = call(residual_kernel, "residual", (species, slab_rows // peers), shares, panel)
-    return update.reshape(rhs.shape), residual
+        landing_kernel, "landing", VMEM((rows, slots), BF16), own, group_map,
+        scratch=[VMEM((peers, rows), I32), VMEM((rows, 1), F32)],
+    )
+    if POOL == "yl":
+        incoming, away, landing = lax.optimization_barrier((incoming, away, landing))
+    other = lax.ppermute(away, POOL, [(0, 1), (1, 0)])
+    panel = call(
+        assemble_kernel, "assemble", VMEM((species, slots), F32), vm(incoming), vm(landing)
+    )
+    if RING:
+        panels = lax.all_gather(panel, GATHER, axis=0)
+    else:
+        panels = lax.all_to_all(jnp.broadcast_to(panel[None], (levels, species, slots)), GATHER, 0, 0)
+    partial = call(
+        product_kernel, "product", VMEM((2 * peers, 8, 128), F32),
+        side, vm(panels), vm(hi), vm(lo), vm(other), vm(panel), vm(landing),
+    )
+    shares = lax.all_to_all(partial, (POOL,) + SUB, 0, 0)
+    update, residual = call(
+        back_kernel,
+        "back",
+        [
+            jax.ShapeDtypeStruct((subs, species * blocks, width), F32),
+            jax.ShapeDtypeStruct((slab_rows // peers, species), F32),
+        ],
+        side, vm(shares), vm(panel), vm(order), vm(whi), vm(wlo), rhs2, inverse,
+        scratch=[pairs],
+    )
+    return update.reshape(rhs.shape), residual.T
 
 
 def solution(mesh):
-    fine = Mesh(mesh.devices.reshape(16, 2, 4, 2, 2), ("z", "yl", "x", "yh", "c"))
-    blk, sub = ("z", "yl"), SUB
+    fine = Mesh(mesh.devices.reshape(8, 2, 2, 4, 2, 2), ("zh", "zl", "yl", "x", "yh", "c"))
+    blk, sub = ("zh", "zl", "yl"), SUB
     every = blk + sub
     placed = (
         P(every, None, None, None),

time: 105 us -> 71.5 us (0.68)
  blocking collectives: 0 us -> 44.6 us
  waiting for transfers between devices: 32.8 us -> 3.16 us
  starting transfers between devices: 40.9 us -> 12 us
  local copies, waits for them, and re-layouts: 12 us -> 1.76 us
  Pallas kernels: 16.8 us -> 8.77 us
  other arithmetic: 1.43 us -> 0 us
    all_to_all x0 -> x2, blocking collectives: none -> 44.6 us  [the longest x1 27.1 us: per_device(): lax.all_to_all(jnp.broadcast_to(panel[None], (levels, species, slots)), G...]
    all_to_all x3 -> x0, starting transfers between devices: 28.9 us -> none  [the longest x1 14.9 us: per_device(): lax.all_to_all(jnp.broadcast_to(panel[None], (levels, species, slots)), '...]
    all_to_all x3 -> x0, waiting for transfers between devices: 19.2 us -> none  [the longest x1 12.1 us: per_device(): lax.all_to_all(jnp.broadcast_to(panel[None], (levels, species, slots)), '...]
    all_to_all x1, waiting for transfers between devices: 13.7 us -> 3.16 us  [per_device(): incoming = lax.all_to_all(outgoing, SUB, 0, 0)]
    pallas_call x7 -> x6, Pallas kernels: 16.8 us -> 8.77 us  [call(): pl.pallas_call(kernel, out_shape=outs, in_specs=specs, out_specs=[whole]...]
    slice x1 -> x0, local copies, waits for them, and re-layouts: 3.37 us -> none  [per_device(): paired[:, :, 1]]
    reshape x1 -> x0, local copies, waits for them, and re-layouts: 3.03 us -> none  [per_device(): paired = slab.reshape(slab_rows, levels, 2, slots)]
    unnamed x12 -> x8, local copies, waits for them, and re-layouts: 4.16 us -> 1.71 us
  transfers between devices with their start and end apart: 5 -> 2, of which waited for: 4 -> 1; matrix products, arithmetic and copies ran while one was open for 1% -> 0% of each run, Pallas kernels for 15% -> 4%
where the time goes in v2:
time: 71.5 us; the launch traced here: 71.1 us
  blocking collectives  44.6 us (62%)
  starting transfers between devices  12 us (17%)
  Pallas kernels  8.77 us (12%)
  waiting for transfers between devices  3.16 us (4%)
  local copies, waits for them, and re-layouts  1.76 us (2%)
    all_to_all x1, blocking collectives, per_device(): lax.all_to_all(jnp.broadcast_to(panel[None], (levels, species, slots)), G...  27.1 us
    all_to_all x1, blocking collectives, per_device(): shares = lax.all_to_all(partial, (POOL,) + SUB, 0, 0)  17.5 us
    all_to_all x1, starting transfers between devices, per_device(): incoming = lax.all_to_all(outgoing, SUB, 0, 0)  10.1 us
    pallas_call x6, Pallas kernels, call(): pl.pallas_call(kernel, out_shape=outs, in_specs=specs, out_specs=[whole]...  8.77 us
    all_to_all x1, waiting for transfers between devices, per_device(): incoming = lax.all_to_all(outgoing, SUB, 0, 0)  3.16 us
    ppermute x1, starting transfers between devices, per_device(): other = lax.ppermute(away, POOL, [(0, 1), (1, 0)])  1.91 us
    unnamed x8, local copies, waits for them, and re-layouts  1.71 us
  transfers between devices with their start and end apart: 2, of which 1 were waited for; matrix products, arithmetic and copies ran while one was open for 0% of the time, Pallas kernels for 4%

profile of v2, /device:TPU:1, one launch (start us, length us, event | category | flops | bytes accessed | tf_op | source)
XLA Modules:
  0.0 71.1 jit_solution(18042239551571724972)
XLA Ops:
  0.6 3.4 %front.1 = (f32[16,4,128]{2,1,0:T(4,128)}, bf16[512,512]{1,0:T(8,128)(2,1)S(1)}, bf16[256,512]{1,0:T(8,128)(2,1)S(1)}, bf16[256,512]{1,0:T(8,128)(2,1)S(1)}) custom-call(s32[1]{0:T(128)} %bitcast.1.own_ref, s32[1,8192]{1,0:T(1,128)} %map_ref.1, s32[5,512]{1,0:T(8,128)} %cells_hbm.1, f32[5,512]{1,0:T(8,128)} %weights_hbm.1, f32[16,512]{1,0:T(8,128)} %face_hbm.1, ...), custom_call_target="tpu_custom_call" | custom-call | tf_op jit(solution)/shard_map/front/pallas_call | solution.py:301
  4.0 10.1 %all-to-all-start = ((f32[16,4,128]{2,1,0:T(4,128)}), f32[16,4,128]{2,1,0:T(4,128)S(1)}, u32[]{:S(2)}, u32[]{:S(2)}) async-start(f32[16,4,128]{2,1,0:T(4,128)} %get-tuple-element.14), calls=%async_computation | async-start | bytes 65536 | tf_op jit(solution)/shard_map/all_to_all | solution.py:349
  14.2 0.0 copy-start.2
  14.2 0.8 %copy-done.2 = s32[1,8192]{1,0:T(1,128)S(1)} copy-done((s32[1,8192]{1,0:T(1,128)S(1)}, s32[1,8192]{1,0:T(1,128)}, u32[]{:S(2)}) %copy-start.2) | copy-done | bytes 32792
  14.9 0.5 landing.1.landing_ref
  15.4 2.0 %cut.1 = (f32[64,4096]{1,0:T(8,128)S(1)}, bf16[64,4096]{1,0:T(8,128)(2,1)S(1)}, bf16[64,4096]{1,0:T(8,128)(2,1)S(1)}) custom-call(s32[1]{0:T(128)} %bitcast.side_ref, f32[64,8192]{1,0:T(8,128)} %slab_ref.1), custom_call_target="tpu_custom_call" | custom-call | tf_op jit(solution)/shard_map/cut/pallas_call | solution.py:301
  17.4 0.0 copy-start.3
  17.4 1.0 %copy-done.3 = f32[64,4096]{1,0:T(8,128)} copy-done((f32[64,4096]{1,0:T(8,128)}, f32[64,4096]{1,0:T(8,128)S(1)}, u32[]{:S(2)}) %copy-start.3) | copy-done | bytes 1048600
  18.4 0.0 copy-start
  18.4 0.0 copy-start.1
  18.4 3.2 %all-to-all-done.in_ref = f32[16,4,128]{2,1,0:T(4,128)S(1)} async-done(((f32[16,4,128]{2,1,0:T(4,128)}), f32[16,4,128]{2,1,0:T(4,128)S(1)}, u32[]{:S(2)}, u32[]{:S(2)}) %all-to-all-start) | async-done | bytes 32800 | tf_op jit(solution)/shard_map/all_to_all | solution.py:349
  21.5 1.9 %collective-permute-start = (f32[64,4096]{1,0:T(8,128)}, f32[64,4096]{1,0:T(8,128)S(1)}, u32[]{:S(2)}, u32[]{:S(2)}) collective-permute-start(f32[64,4096]{1,0:T(8,128)} %copy-done.3), channel_id=1, source_target_pairs={{0,16},{16,0},{1,17},{17,1},{2,18},{18,2},{3,19},{19,3},{4,20},{20... | collective-permute-start | bytes 3145736 | tf_op jit(solution)/shard_map/ppermute | solution.py:365
  23.5 0.2 assemble.1.panel_ref
  23.7 27.1 %all_to_all.15.panels_ref = f32[16,16,256]{2,1,0:T(8,128)S(1)} all-to-all(f32[16,16,256]{2,1,0:T(8,128)S(1)} %broadcast_in_dim.2), channel_id=1, replica_groups=mesh['zh'=8,'zl'=2,'yl'=2,'x'=4,'yh'=2,'c'=2] {'zh','zl'}, dimensions={0} | all-to-all | bytes 524288 | tf_op jit(solution)/shard_map/all_to_all | solution.py:372
  50.9 0.0 collective-permute-done.other_ref
  50.9 0.8 %product.1 = f32[32,8,128]{2,1,0:T(8,128)S(1)} custom-call(s32[1]{0:T(128)} %bitcast.side_ref, f32[16,16,256]{2,1,0:T(8,128)S(1)} %all_to_all.15.panels_ref, bf16[64,4096]{1,0:T(8,128)(2,1)S(1)} %get-tuple-element.18.hi_ref, bf16[64,4096]{1,0:T(8,128)(2,1)S(1)} %get-tuple-element.19.lo_ref, f32[64,4096]{1,0:T(8,128)S(1)} %collective-permute-done.other_ref, ...), custom_call_target="tpu_custom_call" | custom-call | tf_op jit(solution)/shard_map/product/pallas_call | solution.py:301
  51.7 17.5 %all_to_all.16.in_ref = f32[32,8,128]{2,1,0:T(8,128)S(1)} all-to-all(f32[32,8,128]{2,1,0:T(8,128)S(1)} %product.1), channel_id=1, replica_groups=mesh['zh'=8,'zl'=2,'yl'=2,'x'=4,'yh'=2,'c'=2] {'yl','x','yh','c'}, dimensions={0} | all-to-all | bytes 262144 | tf_op jit(solution)/shard_map/all_to_all | solution.py:377
  69.2 0.0 copy-done
  69.2 0.0 copy-done.1
  69.2 1.9 %back.1 = (f32[8,32,128]{2,1,0:T(8,128)}, f32[4,16]{1,0:T(4,128)}) custom-call(s32[1]{0:T(128)} %bitcast.side_ref, f32[32,8,128]{2,1,0:T(8,128)S(1)} %all_to_all.16.in_ref, f32[16,256]{1,0:T(8,128)S(1)} %assemble.1.panel_ref, bf16[512,512]{1,0:T(8,128)(2,1)S(1)} %get-tuple-element.21.order_ref, bf16[256,512]{1,0:T(8,128)(2,1)S(1)} %get-tuple-element.22.whi_ref, ...), custom_call_target="tpu_custom_call" | custom-call | tf_op jit(solution)/shard_map/back/pallas_call | solution.py:301
  (1 shorter events, 0.0 us)
Async XLA Ops:
  4.0 17.5 %all-to-all-start = ((f32[16,4,128]{2,1,0:T(4,128)}), f32[16,4,128]{2,1,0:T(4,128)S(1)}, u32[]{:S(2)}, u32[]{:S(2)}) async-start(f32[16,4,128]{2,1,0:T(4,128)} %get-tuple-element.14), calls=%async_computation | async-start | bytes 65536 | tf_op jit(solution)/shard_map/all_to_all | solution.py:349
  14.2 0.8 %copy-start.2 = (s32[1,8192]{1,0:T(1,128)S(1)}, s32[1,8192]{1,0:T(1,128)}, u32[]{:S(2)}) copy-start(s32[1,8192]{1,0:T(1,128)} %map_ref.1) | copy-start | bytes 98308
  17.4 1.0 %copy-start.3 = (f32[64,4096]{1,0:T(8,128)}, f32[64,4096]{1,0:T(8,128)S(1)}, u32[]{:S(2)}) copy-start(f32[64,4096]{1,0:T(8,128)S(1)} %get-tuple-element.20) | copy-start | bytes 3145732
  18.4 50.8 %copy-start = (bf16[8,2,128,128]{3,2,1,0:T(8,128)(2,1)S(1)}, bf16[8,2,128,128]{3,2,1,0:T(8,128)(2,1)}, u32[]{:S(2)}) copy-start(bf16[8,2,128,128]{3,2,1,0:T(8,128)(2,1)} %inv_ref.1) | copy-start | bytes 1572868
  18.4 50.8 %copy-start.1 = (bf16[8,16,2,128]{3,2,1,0:T(2,128)(2,1)S(1)}, bf16[8,16,2,128]{3,2,1,0:T(2,128)(2,1)}, u32[]{:S(2)}) copy-start(bf16[8,16,2,128]{3,2,1,0:T(2,128)(2,1)} %param.7) | copy-start | bytes 196612
  21.5 29.3 %collective-permute-start = (f32[64,4096]{1,0:T(8,128)}, f32[64,4096]{1,0:T(8,128)S(1)}, u32[]{:S(2)}, u32[]{:S(2)}) collective-permute-start(f32[64,4096]{1,0:T(8,128)} %copy-done.3), channel_id=1, source_target_pairs={{0,16},{16,0},{1,17},{17,1},{2,18},{18,2},{3,19},{19,3},{4,20},{20... | collective-permute-start | bytes 3145736 | tf_op jit(solution)/shard_map/ppermute | solution.py:365

commit v3 on v2

v3 whole, which is shorter than its diff:
```python
import jax
import jax.numpy as jnp
from jax import lax
from jax.experimental import pallas as pl
from jax.experimental.pallas import tpu as pltpu
from jax.sharding import Mesh
from jax.sharding import PartitionSpec as P

F32, BF16, I32 = jnp.float32, jnp.bfloat16, jnp.int32
NN = (((1,), (0,)), ((), ()))
NT = (((1,), (1,)), ((), ()))
SUB = ("x", "yh", "c")


def mxu(a, b, dims=NN):
    return lax.dot_general(a, b, dims, preferred_element_type=F32)


def halves(x):
    hi = x.astype(BF16)
    return hi, (x - hi.astype(F32)).astype(BF16)


def thirds(x):
    hi = x.astype(BF16)
    rest = x - hi.astype(F32)
    mid = rest.astype(BF16)
    return hi, mid, (rest - mid.astype(F32)).astype(BF16)


def iota(shape, axis):
    return lax.broadcasted_iota(I32, shape, axis)


def select_rows(x, onehot, dims):
    n = x.shape[0]
    y = mxu(jnp.concatenate(thirds(x), axis=0), onehot, dims)
    return y[:n] + y[n : 2 * n] + y[2 * n :]


def ranks(hit):
    n, rows = hit.shape
    hit = hit.astype(F32).astype(BF16)
    tiles = [hit[:, t : t + 128] for t in range(0, rows, 128)]
    row, col = iota((128, 256), 0), iota((128, 256), 1)
    ahead = ((row < col) | (col >= 128)).astype(F32).astype(BF16)
    counts = mxu(jnp.concatenate(tiles, axis=0), ahead)
    out, base = [], jnp.zeros((n, 128), F32)
    for t in range(len(tiles)):
        part = counts[t * n : (t + 1) * n]
        out.append(part[:, :128] + base)
        base = base + part[:, 128:]
    return jnp.concatenate(out, axis=1)


def row_numbers():
    return iota((256, 128), 0).astype(F32).astype(BF16)


def pack(x, store):
    lane = iota((4, 128), 1) // 32
    for u in range(x.shape[1] // 128):
        tile = x[:, u * 128 : (u + 1) * 128]
        turned = [tile] + [pltpu.roll(tile, k * 32, 1) for k in range(1, 4)]
        for v in range(4):
            block = turned[(0 - v) % 4][0:4]
            for b in range(1, 4):
                block = jnp.where(lane == b, turned[(b - v) % 4][4 * b : 4 * b + 4], block)
            store(4 * u + v, block)


def unpack(load, peers):
    lane = iota((4, 128), 1) // 32
    tiles = []
    for u in range(peers // 4):
        blocks = [load(4 * u + v) for v in range(4)]
        turned = [[blk] + [pltpu.roll(blk, k * 32, 1) for k in range(1, 4)] for blk in blocks]
        rows = []
        for b in range(4):
            part = turned[0][(0 - b) % 4]
            for v in range(1, 4):
                part = jnp.where(lane == v, turned[v][(v - b) % 4], part)
            rows.append(part)
        tiles.append(jnp.concatenate(rows, axis=0))
    return jnp.concatenate(tiles, axis=1)


def send_place(mapped, peers, slots):
    rows = mapped.shape[1]
    target = mapped // slots
    hit = iota((peers, rows), 0) == target
    rank = jnp.sum(jnp.where(hit, ranks(hit), 0.0), axis=0, keepdims=True)
    return target.astype(F32) * (rows // peers) + rank


def send_order(place, number, store):
    rows = place.shape[1]
    one, zero = jnp.ones((), BF16), jnp.zeros((), BF16)
    for h in range(0, rows, 256):
        inside = (place >= h) & (place < h + 256)
        local = jnp.where(inside, place - h, -1.0).astype(BF16)
        for t in range(0, rows, 128):
            store(h, t, jnp.where(number == local[:, t : t + 128], one, zero))


def coupling(cells, weights, number, store):
    coupled, rows = cells.shape
    cell = [cells[c : c + 1, :].astype(F32) for c in range(coupled)]
    weight = [weights[c : c + 1, :] for c in range(coupled)]
    for c in range(1, coupled):
        for e in range(c):
            same = cell[c] == cell[e]
            weight[e] = weight[e] + jnp.where(same, weight[c], 0.0)
            cell[c] = jnp.where(same, -1.0, cell[c])
    cell = [x.astype(BF16) for x in cell]
    parts = [halves(x) for x in weight]
    for t in range(0, rows, 128):
        high = low = jnp.zeros((256, 128), BF16)
        for c in range(coupled):
            here = number == cell[c][:, t : t + 128]
            high = jnp.where(here, parts[c][0][:, t : t + 128], high)
            low = jnp.where(here, parts[c][1][:, t : t + 128], low)
        store(t, high, low)


def solve(x, inv_ref, d):
    odd = iota((x.shape[0], 128), 0) % 2 == 1
    return jnp.where(odd, mxu(x, inv_ref[d, 1], NT), mxu(x, inv_ref[d, 0], NT))


def front_kernel(
    own_ref, side_ref, map_hbm, cells_hbm, weights_hbm, face_hbm, rhs_hbm, inv_hbm, slab_hbm,
    out_ref, place_ref, whi_ref, wlo_ref, map_ref, mine_ref, away_hbm,
    sums, order_ref, away_ref, cells_ref, weights_ref, face_ref, rhs_ref, inv_ref, sems, cuts,
):
    subs, twice = rhs_ref.shape[0], rhs_ref.shape[1]
    rows = face_ref.shape[1]
    peers = out_ref.shape[0]
    slots = rows // 2
    copies = [
        pltpu.make_async_copy(source, target, sems.at[i])
        for i, (source, target) in enumerate(
            (
                (map_hbm, map_ref),
                (cells_hbm, cells_ref),
                (weights_hbm, weights_ref),
                (face_hbm, face_ref),
                (rhs_hbm, rhs_ref),
                (inv_hbm, inv_ref),
            )
        )
    ]
    for copy in copies:
        copy.start()
    side = side_ref[0]
    slices = []
    for j in range(away_hbm.shape[1] // slots):
        here = pl.ds(j * slots, slots)
        for i, (member, target) in enumerate(((1 - side, away_ref), (side, mine_ref))):
            there = pl.ds(pl.multiple_of((2 * j + member) * slots, 128), slots)
            copy = pltpu.make_async_copy(slab_hbm.at[:, there], target.at[:, here], cuts.at[i, j])
            copy.start()
            slices.append(copy)
    number = row_numbers()
    for copy in copies[:3]:
        copy.wait()

    def order_block(h, t, block):
        order_ref[h : h + 256, t : t + 128] = block

    def coupling_block(t, high, low):
        whi_ref[:, t : t + 128] = high
        wlo_ref[:, t : t + 128] = low

    mapped = map_ref[:, pl.ds(pl.multiple_of(own_ref[0] * rows, 128), rows)]
    place = send_place(mapped, peers, slots)
    place_ref[...] = place
    send_order(place, number, order_block)
    for copy in slices[::2]:
        copy.wait()
    leaving = pltpu.make_async_copy(away_ref, away_hbm, sems.at[6])
    leaving.start()
    coupling(cells_ref[...], weights_ref[...], number, coupling_block)
    for copy in copies[3:]:
        copy.wait()
    for copy in slices[1::2]:
        copy.wait()
    odd = iota((twice, 128), 0) % 2 == 1
    lane = iota((twice, 128), 1)
    for t in range(subs // 2):
        parts = []
        for d in (2 * t, 2 * t + 1):
            y = solve(rhs_ref[d], inv_ref, d)
            parts.append(
                jnp.concatenate([jnp.where(odd, 0.0, y), jnp.where(odd, y, 0.0)], axis=1)
            )
        hi, lo = halves(jnp.concatenate(parts, axis=0))
        cols = slice(t * 128, (t + 1) * 128)
        z = mxu(jnp.concatenate([hi, lo], axis=0), whi_ref[:, cols])
        z = z[: 2 * twice] + z[2 * twice :] + mxu(hi, wlo_ref[:, cols])
        sums[t] = jnp.where(lane < 64, z[:twice], z[twice:])
    half = twice // 2
    faces = [
        face_ref[:, t * 128 : (t + 1) * 128]
        - (sums[t, pl.ds(0, half, stride=2), :] + sums[t, pl.ds(1, half, stride=2), :])
        for t in range(subs // 2)
    ]
    outgoing = select_rows(jnp.concatenate(faces, axis=1), order_ref[...], NT)

    def store(t, block):
        out_ref[t] = block

    pack(outgoing, store)
    leaving.wait()


def landing_kernel(own_ref, map_ref, out_ref, targets, slots_of):
    peers = targets.shape[0]
    rows, slots = out_ref.shape
    for p in range(peers):
        targets[p : p + 1, :] = map_ref[:, p * rows : (p + 1) * rows]
    hit = targets[...] // slots == own_ref[0]
    key = jnp.where(hit, ranks(hit).astype(I32), -1)
    slot = (targets[...] % slots).astype(F32)
    per = rows // peers
    for p in range(peers):
        mine = iota((per, rows), 0) == key[p : p + 1, :]
        slots_of[p * per : (p + 1) * per, :] = jnp.sum(
            jnp.where(mine, slot[p : p + 1, :], 0.0), axis=1, keepdims=True
        )
    column = slots_of[...].astype(I32)
    out_ref[...] = (iota((rows, slots), 1) == column).astype(F32).astype(BF16)


def assemble_kernel(in_ref, landing_ref, out_ref):
    incoming = unpack(lambda t: in_ref[t], in_ref.shape[0])
    out_ref[...] = select_rows(incoming, landing_ref[...], NN)


def product_kernel(
    side_ref, panels_ref, mine_ref, other_ref, panel_ref, landing_ref, out_ref
):
    count, species, slots = panels_ref.shape
    rows = mine_ref.shape[0]
    peers = out_ref.shape[0] // 2
    side = side_ref[0]
    total = jnp.zeros((2 * rows, 2 * species), F32)
    low = jnp.zeros((2 * rows, species), F32)
    for j in range(count):
        cols = slice(j * slots, (j + 1) * slots)
        shi, slo = halves(jnp.concatenate([mine_ref[:, cols], other_ref[:, cols]], axis=0))
        phi, plo = halves(panels_ref[j])
        total += mxu(shi, jnp.concatenate([phi, plo], axis=0), NT)
        low += mxu(slo, phi, NT)
    result = total[:, :species] + total[:, species:] + low
    result = jnp.concatenate([result, jnp.zeros((2 * rows, 128 - species), F32)], axis=1)
    mine, other = side * peers, (1 - side) * peers
    per = rows // peers
    nothing = jnp.zeros((4, 128), F32)
    for p in range(peers):
        out_ref[mine + p, 0:per, :] = result[p * per : (p + 1) * per]
        out_ref[other + p, 0:per, :] = result[rows + p * per : rows + (p + 1) * per]
        out_ref[other + p, per : per + 4, :] = nothing

    def store(t, block):
        out_ref[mine + t, per : per + 4, :] = block

    pack(select_rows(panel_ref[...], landing_ref[...], NT), store)


def back_kernel(
    side_ref, in_ref, panel_ref, place_ref, whi_ref, wlo_ref, rhs_ref, inv_ref,
    out_ref, residual_ref, twofold, order_ref,
):
    subs, twice = rhs_ref.shape[0], rhs_ref.shape[1]
    peers = in_ref.shape[0] // 2
    per, species = residual_ref.shape
    total = jnp.sum(in_ref[...], axis=0)
    eye = (iota((8, 128), 0) == iota((8, 128), 1)).astype(F32)
    first = lax.dot_general(
        eye, panel_ref[:, :128], NT, precision=lax.Precision.HIGHEST, preferred_element_type=F32
    )
    residual_ref[...] = (first - total[:, :species])[:per]
    mine = side_ref[0] * peers
    returned = unpack(lambda t: in_ref[mine + t, per : per + 4, :], peers)

    def order_block(h, t, block):
        order_ref[h : h + 256, t : t + 128] = block

    send_order(place_ref[...], row_numbers(), order_block)
    values = select_rows(returned, order_ref[...], NN)
    half = twice // 2
    for t in range(subs // 2):
        twofold[t, pl.ds(0, half, stride=2), :] = values[:, t * 128 : (t + 1) * 128]
        twofold[t, pl.ds(1, half, stride=2), :] = values[:, t * 128 : (t + 1) * 128]
    odd = iota((twice, 128), 0) % 2 == 1
    lane = iota((twice, 128), 1)
    for t in range(subs // 2):
        cols = slice(t * 128, (t + 1) * 128)
        v = twofold[t]
        hi, lo = halves(
            jnp.concatenate([jnp.where(lane < 64, v, 0.0), jnp.where(lane < 64, 0.0, v)], axis=0)
        )
        z = mxu(jnp.concatenate([hi, lo], axis=0), whi_ref[:, cols], NT)
        z = z[: 2 * twice] + z[2 * twice :] + mxu(hi, wlo_ref[:, cols], NT)
        for i, d in enumerate((2 * t, 2 * t + 1)):
            part = z[i * twice : (i + 1) * twice]
            correction = jnp.where(odd, part[:, 128:], part[:, :128])
            reduced = (rhs_ref[d].astype(F32) - correction).astype(BF16)
            out_ref[d] = solve(reduced, inv_ref, d)


POOL = "yl"
GATHER = ("zh", "zl")
VMEM = pltpu.VMEM


def vm(x):
    return pltpu.with_memory_space_constraint(x, pltpu.VMEM)


def call(kernel, outs, *args, scratch=(), hbm=(), out_hbm=()):
    spaces = [
        pltpu.SMEM if a.ndim == 1 else pltpu.HBM if i in hbm else pltpu.VMEM
        for i, a in enumerate(args)
    ]
    args = [
        pltpu.with_memory_space_constraint(a, pltpu.HBM) if i in hbm else a
        for i, a in enumerate(args)
    ]
    return pl.pallas_call(
        kernel,
        out_shape=outs,
        in_specs=[pl.BlockSpec(memory_space=space) for space in spaces],
        out_specs=[
            pl.BlockSpec(memory_space=pltpu.HBM if i in out_hbm else pltpu.VMEM)
            for i in range(len(outs))
        ],
        scratch_shapes=scratch,
        compiler_params=pltpu.CompilerParams(vmem_limit_bytes=16 << 20),
    )(*args)


def per_device(rhs, inverse, rhs_face, cells, weights, group_map, slab):
    subs, species, blocks, width = rhs.shape
    rows = rhs_face.shape[1]
    slots = rows // 2
    peers = lax.axis_size(SUB)
    levels = lax.axis_size(GATHER)
    slab_rows = slab.shape[0]
    own = lax.axis_index(SUB).astype(I32).reshape(1)
    side = lax.axis_index(POOL).astype(I32).reshape(1)
    rhs2 = rhs.reshape(subs, species * blocks, width)
    pairs = VMEM((subs // 2, species * blocks, 128), F32)

    half = levels * slots
    outgoing, place, whi, wlo, mapped, mine, away = call(
        front_kernel,
        [
            VMEM((peers, 4, 128), F32),
            VMEM((1, rows), F32),
            VMEM((blocks * width, rows), BF16),
            VMEM((blocks * width, rows), BF16),
            VMEM(group_map.shape, I32),
            VMEM((slab_rows, half), F32),
            pltpu.HBM((slab_rows, half), F32),
        ],
        own, side, group_map, cells, weights, rhs_face, rhs2, inverse, slab,
        scratch=[
            pairs,
            VMEM((rows, rows), BF16),
            VMEM((slab_rows, half), F32),
            VMEM(cells.shape, I32),
            VMEM(weights.shape, F32),
            VMEM(rhs_face.shape, F32),
            VMEM(rhs2.shape, BF16),
            VMEM(inverse.shape, BF16),
            pltpu.SemaphoreType.DMA((7,)),
            pltpu.SemaphoreType.DMA((2, levels)),
        ],
        hbm=range(2, 9),
        out_hbm=(6,),
    )
    incoming = lax.all_to_all(outgoing, SUB, 0, 0)
    other = lax.ppermute(away, POOL, [(0, 1), (1, 0)])
    (landing,) = call(
        landing_kernel, [VMEM((rows, slots), BF16)], own, vm(mapped),
        scratch=[VMEM((peers, rows), I32), VMEM((rows, 1), F32)],
    )
    (panel,) = call(assemble_kernel, [VMEM((species, slots), F32)], vm(incoming), vm(landing))
    panels = lax.all_to_all(jnp.broadcast_to(panel[None], (levels, species, slots)), GATHER, 0, 0)
    (partial,) = call(
        product_kernel, [VMEM((2 * peers, 8, 128), F32)],
        side, vm(panels), vm(mine), vm(other), vm(panel), vm(landing),
    )
    shares = lax.all_to_all(partial, (POOL,) + SUB, 0, 0)
    update, residual = call(
        back_kernel,
        [
            jax.ShapeDtypeStruct((subs, species * blocks, width), F32),
            jax.ShapeDtypeStruct((slab_rows // peers, species), F32),
        ],
        side, vm(shares), vm(panel), vm(place), vm(whi), vm(wlo), rhs2, inverse,
        scratch=[
            pairs,
            VMEM((rows, rows), BF16),
        ],
    )
    return update.reshape(rhs.shape), residual.T


def solution(mesh):
    fine = Mesh(mesh.devices.reshape(8, 2, 2, 4, 2, 2), ("zh", "zl", "yl", "x", "yh", "c"))
    blk, sub = ("zh", "zl", "yl"), SUB
    every = blk + sub
    placed = (
        P(every, None, None, None),
        P(every, None, None, None),
        P(None, every),
        P(None, every),
        P(None, every),
        P(blk, None),
        P(blk, sub),
    )

    return jax.shard_map(
        per_device,
        mesh=fine,
        in_specs=placed,
        out_specs=(P(every, None, None, None), P(None, every)),
        check_vma=False,
    )
```

time: 71.5 us -> 84.7 us (1.18)
  waiting for transfers between devices: 3.16 us -> 18.3 us
  local copies, waits for them, and re-layouts: 1.76 us -> 0.06 us
  Pallas kernels: 8.77 us -> 7.49 us
  blocking collectives: 44.6 us -> 45.8 us
    all_to_all x1, waiting for transfers between devices: 3.16 us -> 18.3 us  [per_device(): incoming = lax.all_to_all(outgoing, SUB, 0, 0)]
    ppermute x1, starting transfers between devices: 1.91 us -> 4.02 us  [per_device(): other = lax.ppermute(away, POOL, [(0, 1), (1, 0)])]
    all_to_all x1, starting transfers between devices: 10.1 us -> 8.03 us  [per_device(): incoming = lax.all_to_all(outgoing, SUB, 0, 0)]
    unnamed x8 -> x4, local copies, waits for them, and re-layouts: 1.71 us -> 0.01 us
    all_to_all x1, blocking collectives: 27.1 us -> 28.7 us  [per_device(): lax.all_to_all(jnp.broadcast_to(panel[None], (levels, species, slots)), G...]
    pallas_call x6 -> x5, Pallas kernels: 8.77 us -> 7.49 us  [call(): pl.pallas_call(kernel, out_shape=outs, in_specs=[pl.BlockSpec(memory_spac...]
  transfers between devices with their start and end apart: 2 -> 2, of which waited for: 1 -> 1; matrix products, arithmetic and copies ran while one was open for 0% -> 0% of each run, Pallas kernels for 4% -> 1%
where the time goes in v3:
time: 84.7 us; the launch traced here: 84.4 us
  blocking collectives  45.8 us (54%)
  waiting for transfers between devices  18.3 us (22%)
  starting transfers between devices  12.1 us (14%)
  Pallas kernels  7.49 us (9%)
    all_to_all x1, blocking collectives, per_device(): lax.all_to_all(jnp.broadcast_to(panel[None], (levels, species, slots)), G...  28.7 us
    all_to_all x1, waiting for transfers between devices, per_device(): incoming = lax.all_to_all(outgoing, SUB, 0, 0)  18.3 us
    all_to_all x1, blocking collectives, per_device(): shares = lax.all_to_all(partial, (POOL,) + SUB, 0, 0)  17.1 us
    all_to_all x1, starting transfers between devices, per_device(): incoming = lax.all_to_all(outgoing, SUB, 0, 0)  8.03 us
    pallas_call x5, Pallas kernels, call(): pl.pallas_call(kernel, out_shape=outs, in_specs=[pl.BlockSpec(memory_spac...  7.49 us
    ppermute x1, starting transfers between devices, per_device(): other = lax.ppermute(away, POOL, [(0, 1), (1, 0)])  4.02 us
  transfers between devices with their start and end apart: 2, of which 1 were waited for; matrix products, arithmetic and copies ran while one was open for 0% of the time, Pallas kernels for 1%

profile of v3, /device:TPU:1, one launch (start us, length us, event | category | flops | bytes accessed | tf_op | source)
XLA Modules:
  0.0 84.4 jit_solution(2610244230026629484)
XLA Ops:
  0.6 4.1 %shard_map.86 = (f32[16,4,128]{2,1,0:T(4,128)}, f32[1,512]{1,0:T(1,128)S(1)}, bf16[256,512]{1,0:T(8,128)(2,1)S(1)}, bf16[256,512]{1,0:T(8,128)(2,1)S(1)}, s32[1,...) custom-call(s32[1]{0:T(128)} %bitcast.1.own_ref, s32[1]{0:T(128)} %bitcast.side_ref, ...), custom_call_target="tpu_custom_call" | custom-call | tf_op jit(solution)/shard_map/pallas_call | solution.py:331
  4.7 4.0 %collective-permute-start = (f32[64,4096]{1,0:T(8,128)}, f32[64,4096]{1,0:T(8,128)S(1)}, u32[]{:S(2)}, u32[]{:S(2)}) collective-permute-start(f32[64,4096]{1,0:T(8,128)} %get-tuple-element.14), channel_id=1, source_target_pairs={{0,16},{16,0},{1,17},{17,1},{2,18},{18,2},{3,19},{19,3},{4,20},{20... | collective-permute-start | bytes 3145736 | tf_op jit(solution)/shard_map/ppermute | solution.py:385
  8.8 8.0 %all-to-all-start = ((f32[16,4,128]{2,1,0:T(4,128)}), f32[16,4,128]{2,1,0:T(4,128)S(1)}, u32[]{:S(2)}, u32[]{:S(2)}) async-start(f32[16,4,128]{2,1,0:T(4,128)} %get-tuple-element.11), calls=%async_computation | async-start | bytes 65536 | tf_op jit(solution)/shard_map/all_to_all | solution.py:384
  16.8 0.5 shard_map.87.landing_ref
  17.2 0.0 copy-start
  17.3 0.0 copy-start.1
  17.3 18.3 %all-to-all-done.in_ref = f32[16,4,128]{2,1,0:T(4,128)S(1)} async-done(((f32[16,4,128]{2,1,0:T(4,128)}), f32[16,4,128]{2,1,0:T(4,128)S(1)}, u32[]{:S(2)}, u32[]{:S(2)}) %all-to-all-start) | async-done | bytes 32800 | tf_op jit(solution)/shard_map/all_to_all | solution.py:384
  35.6 0.2 shard_map.88.panel_ref
  35.9 28.7 %all_to_all.15.panels_ref = f32[16,16,256]{2,1,0:T(8,128)S(1)} all-to-all(f32[16,16,256]{2,1,0:T(8,128)S(1)} %broadcast_in_dim.2), channel_id=1, replica_groups=mesh['zh'=8,'zl'=2,'yl'=2,'x'=4,'yh'=2,'c'=2] {'zh','zl'}, dimensions={0} | all-to-all | bytes 524288 | tf_op jit(solution)/shard_map/all_to_all | solution.py:391
  64.6 0.0 collective-permute-done.other_ref
  64.6 0.8 shard_map.89
  65.4 17.1 %all_to_all.16.in_ref = f32[32,8,128]{2,1,0:T(8,128)S(1)} all-to-all(f32[32,8,128]{2,1,0:T(8,128)S(1)} %shard_map.89), channel_id=1, replica_groups=mesh['zh'=8,'zl'=2,'yl'=2,'x'=4,'yh'=2,'c'=2] {'yl','x','yh','c'}, dimensions={0} | all-to-all | bytes 262144 | tf_op jit(solution)/shard_map/all_to_all | solution.py:396
  82.5 0.0 copy-done
  82.5 0.0 copy-done.1
  82.5 1.9 %shard_map.90 = (f32[8,32,128]{2,1,0:T(8,128)}, f32[4,16]{1,0:T(4,128)}) custom-call(s32[1]{0:T(128)} %bitcast.side_ref, f32[32,8,128]{2,1,0:T(8,128)S(1)} %all_to_all.16.in_ref, f32[16,256]{1,0:T(8,128)S(1)} %shard_map.88.panel_ref, f32[1,512]{1,0:T(1,128)S(1)} %get-tuple-element.15.place_ref, bf16[256,512]{1,0:T(8,128)(2,1)S(1)} %get-tuple-element.16.whi_ref, ...), custom_call_target="tpu_custom_call" | custom-call | tf_op jit(solution)/shard_map/pallas_call | solution.py:331
  (1 shorter events, 0.0 us)
Async XLA Ops:
  4.7 59.9 %collective-permute-start = (f32[64,4096]{1,0:T(8,128)}, f32[64,4096]{1,0:T(8,128)S(1)}, u32[]{:S(2)}, u32[]{:S(2)}) collective-permute-start(f32[64,4096]{1,0:T(8,128)} %get-tuple-element.14), channel_id=1, source_target_pairs={{0,16},{16,0},{1,17},{17,1},{2,18},{18,2},{3,19},{19,3},{4,20},{20... | collective-permute-start | bytes 3145736 | tf_op jit(solution)/shard_map/ppermute | solution.py:385
  8.8 26.9 %all-to-all-start = ((f32[16,4,128]{2,1,0:T(4,128)}), f32[16,4,128]{2,1,0:T(4,128)S(1)}, u32[]{:S(2)}, u32[]{:S(2)}) async-start(f32[16,4,128]{2,1,0:T(4,128)} %get-tuple-element.11), calls=%async_computation | async-start | bytes 65536 | tf_op jit(solution)/shard_map/all_to_all | solution.py:384
  17.2 65.3 %copy-start = (bf16[8,2,128,128]{3,2,1,0:T(8,128)(2,1)S(1)}, bf16[8,2,128,128]{3,2,1,0:T(8,128)(2,1)}, u32[]{:S(2)}) copy-start(bf16[8,2,128,128]{3,2,1,0:T(8,128)(2,1)} %inv_ref.1) | copy-start | bytes 1572868
  17.3 65.3 %copy-start.1 = (bf16[8,16,2,128]{3,2,1,0:T(2,128)(2,1)S(1)}, bf16[8,16,2,128]{3,2,1,0:T(2,128)(2,1)}, u32[]{:S(2)}) copy-start(bf16[8,16,2,128]{3,2,1,0:T(2,128)(2,1)} %param.7) | copy-start | bytes 196612

commit v4 on v3

--- a/solution.py
+++ b/solution.py
@@ -130,8 +130,8 @@
 
 def front_kernel(
     own_ref, side_ref, map_hbm, cells_hbm, weights_hbm, face_hbm, rhs_hbm, inv_hbm, slab_hbm,
-    out_ref, place_ref, whi_ref, wlo_ref, map_ref, mine_ref, away_hbm,
-    sums, order_ref, away_ref, cells_ref, weights_ref, face_ref, rhs_ref, inv_ref, sems, cuts,
+    out_ref, place_ref, whi_ref, wlo_ref, landing_ref, mine_ref, away_hbm,
+    targets, slots_of, map_ref, sums, order_ref, away_ref, cells_ref, weights_ref, face_ref, rhs_ref, inv_ref, sems, cuts,
 ):
     subs, twice = rhs_ref.shape[0], rhs_ref.shape[1]
     rows = face_ref.shape[1]
@@ -154,13 +154,10 @@
         copy.start()
     side = side_ref[0]
     slices = []
-    for j in range(away_hbm.shape[1] // slots):
-        here = pl.ds(j * slots, slots)
-        for i, (member, target) in enumerate(((1 - side, away_ref), (side, mine_ref))):
-            there = pl.ds(pl.multiple_of((2 * j + member) * slots, 128), slots)
-            copy = pltpu.make_async_copy(slab_hbm.at[:, there], target.at[:, here], cuts.at[i, j])
-            copy.start()
-            slices.append(copy)
+    for i, (member, target) in enumerate(((1 - side, away_ref), (side, mine_ref))):
+        copy = pltpu.make_async_copy(slab_hbm.at[:, :, member], target, cuts.at[i])
+        copy.start()
+        slices.append(copy)
     number = row_numbers()
     for copy in copies[:3]:
         copy.wait()
@@ -182,8 +179,6 @@
     leaving.start()
     coupling(cells_ref[...], weights_ref[...], number, coupling_block)
     for copy in copies[3:]:
-        copy.wait()
-    for copy in slices[1::2]:
         copy.wait()
     odd = iota((twice, 128), 0) % 2 == 1
     lane = iota((twice, 128), 1)
@@ -211,15 +206,17 @@
         out_ref[t] = block
 
     pack(outgoing, store)
+    landing_of(own_ref[0], map_ref, landing_ref, targets, slots_of)
     leaving.wait()
-
-
-def landing_kernel(own_ref, map_ref, out_ref, targets, slots_of):
+    slices[1].wait()
+
+
+def landing_of(own, map_ref, out_ref, targets, slots_of):
     peers = targets.shape[0]
     rows, slots = out_ref.shape
     for p in range(peers):
         targets[p : p + 1, :] = map_ref[:, p * rows : (p + 1) * rows]
-    hit = targets[...] // slots == own_ref[0]
+    hit = targets[...] // slots == own
     key = jnp.where(hit, ranks(hit).astype(I32), -1)
     slot = (targets[...] % slots).astype(F32)
     per = rows // peers
@@ -241,14 +238,17 @@
     side_ref, panels_ref, mine_ref, other_ref, panel_ref, landing_ref, out_ref
 ):
     count, species, slots = panels_ref.shape
-    rows = mine_ref.shape[0]
+    rows = mine_ref.shape[0] * 8
     peers = out_ref.shape[0] // 2
     side = side_ref[0]
     total = jnp.zeros((2 * rows, 2 * species), F32)
     low = jnp.zeros((2 * rows, species), F32)
     for j in range(count):
-        cols = slice(j * slots, (j + 1) * slots)
-        shi, slo = halves(jnp.concatenate([mine_ref[:, cols], other_ref[:, cols]], axis=0))
+        tiles = [
+            jnp.concatenate([ref[:, j, k].reshape(rows, 128) for ref in (mine_ref, other_ref)], axis=0)
+            for k in range(slots // 128)
+        ]
+        shi, slo = halves(jnp.concatenate(tiles, axis=1))
         phi, plo = halves(panels_ref[j])
         total += mxu(shi, jnp.concatenate([phi, plo], axis=0), NT)
         low += mxu(slo, phi, NT)
@@ -353,40 +353,41 @@
     rhs2 = rhs.reshape(subs, species * blocks, width)
     pairs = VMEM((subs // 2, species * blocks, 128), F32)
 
-    half = levels * slots
-    outgoing, place, whi, wlo, mapped, mine, away = call(
+    half = (slab_rows // 8, levels, slots // 128, 8, 128)
+    tiled = slab.reshape(slab_rows // 8, 8, 2 * levels * slots // 128, 128)
+    tiled = jnp.transpose(tiled, (0, 2, 1, 3)).reshape(half[:2] + (2,) + half[2:])
+    outgoing, place, whi, wlo, landing, mine, away = call(
         front_kernel,
         [
             VMEM((peers, 4, 128), F32),
             VMEM((1, rows), F32),
             VMEM((blocks * width, rows), BF16),
             VMEM((blocks * width, rows), BF16),
+            VMEM((rows, slots), BF16),
+            VMEM(half, F32),
+            pltpu.HBM(half, F32),
+        ],
+        own, side, group_map, cells, weights, rhs_face, rhs2, inverse, tiled,
+        scratch=[
+            VMEM((peers, rows), I32),
+            VMEM((rows, 1), F32),
             VMEM(group_map.shape, I32),
-            VMEM((slab_rows, half), F32),
-            pltpu.HBM((slab_rows, half), F32),
-        ],
-        own, side, group_map, cells, weights, rhs_face, rhs2, inverse, slab,
-        scratch=[
             pairs,
             VMEM((rows, rows), BF16),
-            VMEM((slab_rows, half), F32),
+            VMEM(half, F32),
             VMEM(cells.shape, I32),
             VMEM(weights.shape, F32),
             VMEM(rhs_face.shape, F32),
             VMEM(rhs2.shape, BF16),
             VMEM(inverse.shape, BF16),
             pltpu.SemaphoreType.DMA((7,)),
-            pltpu.SemaphoreType.DMA((2, levels)),
+            pltpu.SemaphoreType.DMA((2,)),
         ],
         hbm=range(2, 9),
         out_hbm=(6,),
     )
     incoming = lax.all_to_all(outgoing, SUB, 0, 0)
     other = lax.ppermute(away, POOL, [(0, 1), (1, 0)])
-    (landing,) = call(
-        landing_kernel, [VMEM((rows, slots), BF16)], own, vm(mapped),
-        scratch=[VMEM((peers, rows), I32), VMEM((rows, 1), F32)],
-    )
     (panel,) = call(assemble_kernel, [VMEM((species, slots), F32)], vm(incoming), vm(landing))
     panels = lax.all_to_all(jnp.broadcast_to(panel[None], (levels, species, slots)), GATHER, 0, 0)
     (partial,) = call(

time: 84.7 us -> 83.7 us (0.988)
  blocking collectives: 45.8 us -> 72.6 us
  waiting for transfers between devices: 18.3 us -> 0.01 us
  starting transfers between devices: 12.1 us -> 4.02 us
  Pallas kernels: 7.49 us -> 6.08 us
    all_to_all x0 -> x1, blocking collectives: none -> 26.8 us  [per_device(): incoming = lax.all_to_all(outgoing, SUB, 0, 0)]
    all_to_all x1 -> x0, waiting for transfers between devices: 18.3 us -> none  [per_device(): incoming = lax.all_to_all(outgoing, SUB, 0, 0)]
    all_to_all x1 -> x0, starting transfers between devices: 8.03 us -> none  [per_device(): incoming = lax.all_to_all(outgoing, SUB, 0, 0)]
    pallas_call x5 -> x4, Pallas kernels: 7.49 us -> 6.08 us  [call(): pl.pallas_call(kernel, out_shape=outs, in_specs=[pl.BlockSpec(memory_spac...]
  transfers between devices with their start and end apart: 2 -> 1, of which waited for: 1 -> 0; matrix products, arithmetic and copies ran while one was open for 0% -> 0% of each run, Pallas kernels for 1% -> 0%
where the time goes in v4:
time: 83.7 us; the launch traced here: 83.4 us
  blocking collectives  72.6 us (87%)
  Pallas kernels  6.08 us (7%)
  starting transfers between devices  4.02 us (5%)
    all_to_all x1, blocking collectives, per_device(): lax.all_to_all(jnp.broadcast_to(panel[None], (levels, species, slots)), G...  28.7 us
    all_to_all x1, blocking collectives, per_device(): incoming = lax.all_to_all(outgoing, SUB, 0, 0)  26.8 us
    all_to_all x1, blocking collectives, per_device(): shares = lax.all_to_all(partial, (POOL,) + SUB, 0, 0)  17 us
    pallas_call x4, Pallas kernels, call(): pl.pallas_call(kernel, out_shape=outs, in_specs=[pl.BlockSpec(memory_spac...  6.08 us
    ppermute x1, starting transfers between devices, per_device(): other = lax.ppermute(away, POOL, [(0, 1), (1, 0)])  4.02 us
  transfers between devices with their start and end apart: 1, of which 0 were waited for; matrix products, arithmetic and copies ran while one was open for 0% of the time, Pallas kernels for 0%

profile of v4, /device:TPU:1, one launch (start us, length us, event | category | flops | bytes accessed | tf_op | source)
XLA Modules:
  0.0 83.4 jit_solution(15997995566403206695)
XLA Ops:
  0.6 3.1 %shard_map.86 = (f32[16,4,128]{2,1,0:T(4,128)S(1)}, f32[1,512]{1,0:T(1,128)S(1)}, bf16[256,512]{1,0:T(8,128)(2,1)S(1)}, bf16[256,512]{1,0:T(8,128)(2,1)S(1)}, bf...) custom-call(s32[1]{0:T(128)} %bitcast.1.own_ref, s32[1]{0:T(128)} %bitcast.side_ref, ...), custom_call_target="tpu_custom_call" | custom-call | tf_op jit(solution)/shard_map/pallas_call | solution.py:331
  3.8 4.0 %collective-permute-start = (f32[8,16,2,8,128]{4,3,2,1,0:T(8,128)}, f32[8,16,2,8,128]{4,3,2,1,0:T(8,128)S(1)}, u32[]{:S(2)}, u32[]{:S(2)}) collective-permute-start(f32[8,16,2,8,128]{4,3,2,1,0:T(8,128)} %get-tuple-element.14), channel_id=1, source_target_pairs={{0,16},{16,0},{1,17},{17,1},{2,18},{18,2},{3,19},{19,3},{4,20},{20... | collective-permute-start | bytes 3145736 | tf_op jit(solution)/shard_map/ppermute | solution.py:390
  7.8 0.0 copy-start
  7.8 0.0 copy-start.1
  7.8 26.8 %all_to_all.15.in_ref = f32[16,4,128]{2,1,0:T(4,128)S(1)} all-to-all(f32[16,4,128]{2,1,0:T(4,128)S(1)} %get-tuple-element.11), channel_id=1, replica_groups=mesh['zh'=8,'zl'=2,'yl'=2,'x'=4,'yh'=2,'c'=2] {'x','yh','c'}, dimensions={0} | all-to-all | bytes 65536 | tf_op jit(solution)/shard_map/all_to_all | solution.py:389
  34.6 0.2 shard_map.87.panel_ref
  34.9 28.7 %all_to_all.16.panels_ref = f32[16,16,256]{2,1,0:T(8,128)S(1)} all-to-all(f32[16,16,256]{2,1,0:T(8,128)S(1)} %broadcast_in_dim.2), channel_id=1, replica_groups=mesh['zh'=8,'zl'=2,'yl'=2,'x'=4,'yh'=2,'c'=2] {'zh','zl'}, dimensions={0} | all-to-all | bytes 524288 | tf_op jit(solution)/shard_map/all_to_all | solution.py:392
  63.6 0.0 collective-permute-done.other_ref
  63.6 0.8 %shard_map.88 = f32[32,8,128]{2,1,0:T(8,128)S(1)} custom-call(s32[1]{0:T(128)} %bitcast.side_ref, f32[16,16,256]{2,1,0:T(8,128)S(1)} %all_to_all.16.panels_ref, f32[8,16,2,8,128]{4,3,2,1,0:T(8,128)S(1)} %get-tuple-element.13.mine_ref, f32[8,16,2,8,128]{4,3,2,1,0:T(8,128)S(1)} %collective-permute-done.other_ref, f32[16,256]{1,0:T(8,128)S(1)} %shard_map.87.panel_ref, ...), custom_call_target="tpu_custom_call" | custom-call | tf_op jit(solution)/shard_map/pallas_call | solution.py:331
  64.5 17.0 %all_to_all.17.in_ref = f32[32,8,128]{2,1,0:T(8,128)S(1)} all-to-all(f32[32,8,128]{2,1,0:T(8,128)S(1)} %shard_map.88), channel_id=1, replica_groups=mesh['zh'=8,'zl'=2,'yl'=2,'x'=4,'yh'=2,'c'=2] {'yl','x','yh','c'}, dimensions={0} | all-to-all | bytes 262144 | tf_op jit(solution)/shard_map/all_to_all | solution.py:397
  81.5 0.0 copy-done
  81.5 0.0 copy-done.1
  81.5 1.9 %shard_map.89 = (f32[8,32,128]{2,1,0:T(8,128)}, f32[4,16]{1,0:T(4,128)}) custom-call(s32[1]{0:T(128)} %bitcast.side_ref, f32[32,8,128]{2,1,0:T(8,128)S(1)} %all_to_all.17.in_ref, f32[16,256]{1,0:T(8,128)S(1)} %shard_map.87.panel_ref, f32[1,512]{1,0:T(1,128)S(1)} %get-tuple-element.15.place_ref, bf16[256,512]{1,0:T(8,128)(2,1)S(1)} %get-tuple-element.16.whi_ref, ...), custom_call_target="tpu_custom_call" | custom-call | tf_op jit(solution)/shard_map/pallas_call | solution.py:331
  (1 shorter events, 0.0 us)
Async XLA Ops:
  3.8 59.9 %collective-permute-start = (f32[8,16,2,8,128]{4,3,2,1,0:T(8,128)}, f32[8,16,2,8,128]{4,3,2,1,0:T(8,128)S(1)}, u32[]{:S(2)}, u32[]{:S(2)}) collective-permute-start(f32[8,16,2,8,128]{4,3,2,1,0:T(8,128)} %get-tuple-element.14), channel_id=1, source_target_pairs={{0,16},{16,0},{1,17},{17,1},{2,18},{18,2},{3,19},{19,3},{4,20},{20... | collective-permute-start | bytes 3145736 | tf_op jit(solution)/shard_map/ppermute | solution.py:390
  7.8 73.7 %copy-start = (bf16[8,2,128,128]{3,2,1,0:T(8,128)(2,1)S(1)}, bf16[8,2,128,128]{3,2,1,0:T(8,128)(2,1)}, u32[]{:S(2)}) copy-start(bf16[8,2,128,128]{3,2,1,0:T(8,128)(2,1)} %inv_ref.1) | copy-start | bytes 1572868
  7.8 73.7 %copy-start.1 = (bf16[8,16,2,128]{3,2,1,0:T(2,128)(2,1)S(1)}, bf16[8,16,2,128]{3,2,1,0:T(2,128)(2,1)}, u32[]{:S(2)}) copy-start(bf16[8,16,2,128]{3,2,1,0:T(2,128)(2,1)} %param.7) | copy-start | bytes 196612

commit v5 on v4

--- a/solution.py
+++ b/solution.py
@@ -203,7 +203,7 @@
     outgoing = select_rows(jnp.concatenate(faces, axis=1), order_ref[...], NT)
 
     def store(t, block):
-        out_ref[t] = block
+        out_ref[position(t, FIRST)] = block
 
     pack(outgoing, store)
     landing_of(own_ref[0], map_ref, landing_ref, targets, slots_of)
@@ -230,7 +230,7 @@
 
 
 def assemble_kernel(in_ref, landing_ref, out_ref):
-    incoming = unpack(lambda t: in_ref[t], in_ref.shape[0])
+    incoming = unpack(lambda t: in_ref[position(t, FIRST)], in_ref.shape[0])
     out_ref[...] = select_rows(incoming, landing_ref[...], NN)
 
 
@@ -245,7 +245,7 @@
     low = jnp.zeros((2 * rows, species), F32)
     for j in range(count):
         tiles = [
-            jnp.concatenate([ref[:, j, k].reshape(rows, 128) for ref in (mine_ref, other_ref)], axis=0)
+            jnp.concatenate([ref[:, LEVELS[j], k].reshape(rows, 128) for ref in (mine_ref, other_ref)], axis=0)
             for k in range(slots // 128)
         ]
         shi, slo = halves(jnp.concatenate(tiles, axis=1))
@@ -254,16 +254,16 @@
         low += mxu(slo, phi, NT)
     result = total[:, :species] + total[:, species:] + low
     result = jnp.concatenate([result, jnp.zeros((2 * rows, 128 - species), F32)], axis=1)
-    mine, other = side * peers, (1 - side) * peers
     per = rows // peers
     nothing = jnp.zeros((4, 128), F32)
     for p in range(peers):
-        out_ref[mine + p, 0:per, :] = result[p * per : (p + 1) * per]
-        out_ref[other + p, 0:per, :] = result[rows + p * per : rows + (p + 1) * per]
-        out_ref[other + p, per : per + 4, :] = nothing
+        mine, other = position(p, LAST, side), position(p, LAST, 1 - side)
+        out_ref[mine, 0:per, :] = result[p * per : (p + 1) * per]
+        out_ref[other, 0:per, :] = result[rows + p * per : rows + (p + 1) * per]
+        out_ref[other, per : per + 4, :] = nothing
 
     def store(t, block):
-        out_ref[mine + t, per : per + 4, :] = block
+        out_ref[position(t, LAST, side), per : per + 4, :] = block
 
     pack(select_rows(panel_ref[...], landing_ref[...], NT), store)
 
@@ -281,8 +281,8 @@
         eye, panel_ref[:, :128], NT, precision=lax.Precision.HIGHEST, preferred_element_type=F32
     )
     residual_ref[...] = (first - total[:, :species])[:per]
-    mine = side_ref[0] * peers
-    returned = unpack(lambda t: in_ref[mine + t, per : per + 4, :], peers)
+    side = side_ref[0]
+    returned = unpack(lambda t: in_ref[position(t, LAST, side), per : per + 4, :], peers)
 
     def order_block(h, t, block):
         order_ref[h : h + 256, t : t + 128] = block
@@ -311,8 +311,18 @@
 
 
 POOL = "yl"
-GATHER = ("zh", "zl")
+GATHER = "z"
+LEVELS = (8, 11, 14, 1, 4, 7, 10, 13, 0, 3, 6, 9, 12, 15, 2, 5)
+FIRST = (10, 11, 14, 15, 6, 7, 8, 9, 2, 12, 3, 13, 4, 5, 0, 1)
+LAST = (10, 11, 26, 27, 14, 15, 30, 31, 6, 7, 22, 24, 23, 25, 28, 29, 2, 8, 3, 9, 18, 20, 19, 21, 12, 13, 4, 5, 16, 17, 0, 1)
 VMEM = pltpu.VMEM
+
+
+def position(t, order, side=0):
+    if len(order) == 16:
+        return order.index(t)
+    near, far = order.index(t), order.index(16 + t)
+    return near + side * (far - near)
 
 
 def vm(x):
@@ -386,15 +396,23 @@
         hbm=range(2, 9),
         out_hbm=(6,),
     )
-    incoming = lax.all_to_all(outgoing, SUB, 0, 0)
+    incoming = lax.all_to_all(outgoing, SUB, 0, 0, axis_index_groups=[list(FIRST)])
     other = lax.ppermute(away, POOL, [(0, 1), (1, 0)])
     (panel,) = call(assemble_kernel, [VMEM((species, slots), F32)], vm(incoming), vm(landing))
-    panels = lax.all_to_all(jnp.broadcast_to(panel[None], (levels, species, slots)), GATHER, 0, 0)
+    panels = lax.all_to_all(
+        jnp.broadcast_to(panel[None], (levels, species, slots)),
+        GATHER,
+        0,
+        0,
+        axis_index_groups=[list(LEVELS)],
+    )
     (partial,) = call(
         product_kernel, [VMEM((2 * peers, 8, 128), F32)],
         side, vm(panels), vm(mine), vm(other), vm(panel), vm(landing),
     )
-    shares = lax.all_to_all(partial, (POOL,) + SUB, 0, 0)
+    shares = lax.all_to_all(
+        partial, (POOL,) + SUB, 0, 0, axis_index_groups=[list(LAST)]
+    )
     update, residual = call(
         back_kernel,
         [
@@ -411,8 +429,8 @@
 
 
 def solution(mesh):
-    fine = Mesh(mesh.devices.reshape(8, 2, 2, 4, 2, 2), ("zh", "zl", "yl", "x", "yh", "c"))
-    blk, sub = ("zh", "zl", "yl"), SUB
+    fine = Mesh(mesh.devices.reshape(16, 2, 4, 2, 2), ("z", "yl", "x", "yh", "c"))
+    blk, sub = ("z", "yl"), SUB
     every = blk + sub
     placed = (
         P(every, None, None, None),

time: 83.7 us -> 79.2 us (0.946)
  blocking collectives: 72.6 us -> 68.1 us
    all_to_all x2, blocking collectives: 43.9 us -> 38 us  [the longest x1 26.8 us: per_device(): lax.all_to_all(outgoing, SUB, 0, 0, axis_index_groups=[list(FIRST)])]
    all_to_all x1, blocking collectives: 28.7 us -> 30.1 us  [per_device(): lax.all_to_all(jnp.broadcast_to(panel[None], (levels, species, slots)), G...]
where the time goes in v5:
time: 79.2 us; the launch traced here: 79 us
  blocking collectives  68.1 us (86%)
  Pallas kernels  6.08 us (8%)
  starting transfers between devices  4.02 us (5%)
    all_to_all x1, blocking collectives, per_device(): lax.all_to_all(jnp.broadcast_to(panel[None], (levels, species, slots)), G...  30.1 us
    all_to_all x1, blocking collectives, per_device(): lax.all_to_all(outgoing, SUB, 0, 0, axis_index_groups=[list(FIRST)])  26.8 us
    all_to_all x1, blocking collectives, per_device(): lax.all_to_all(partial, (POOL,) + SUB, 0, 0, axis_index_groups=[list(LAST)])  11.2 us
    pallas_call x4, Pallas kernels, call(): pl.pallas_call(kernel, out_shape=outs, in_specs=[pl.BlockSpec(memory_spac...  6.08 us
    ppermute x1, starting transfers between devices, per_device(): other = lax.ppermute(away, POOL, [(0, 1), (1, 0)])  4.02 us
  transfers between devices with their start and end apart: 1, of which 0 were waited for; matrix products, arithmetic and copies ran while one was open for 0% of the time, Pallas kernels for 0%

profile of v5, /device:TPU:1, one launch (start us, length us, event | category | flops | bytes accessed | tf_op | source)
XLA Modules:
  0.0 79.0 jit_solution(17770377768404848480)
XLA Ops:
  0.6 3.1 %shard_map.86 = (f32[16,4,128]{2,1,0:T(4,128)S(1)}, f32[1,512]{1,0:T(1,128)S(1)}, bf16[256,512]{1,0:T(8,128)(2,1)S(1)}, bf16[256,512]{1,0:T(8,128)(2,1)S(1)}, bf...) custom-call(s32[1]{0:T(128)} %bitcast.1.own_ref, s32[1]{0:T(128)} %bitcast.side_ref, ...), custom_call_target="tpu_custom_call" | custom-call | tf_op jit(solution)/shard_map/pallas_call | solution.py:341
  3.8 4.0 %collective-permute-start = (f32[8,16,2,8,128]{4,3,2,1,0:T(8,128)}, f32[8,16,2,8,128]{4,3,2,1,0:T(8,128)S(1)}, u32[]{:S(2)}, u32[]{:S(2)}) collective-permute-start(f32[8,16,2,8,128]{4,3,2,1,0:T(8,128)} %get-tuple-element.14), channel_id=1, source_target_pairs={{0,16},{16,0},{1,17},{17,1},{2,18},{18,2},{3,19},{19,3},{4,20},{20... | collective-permute-start | bytes 3145736 | tf_op jit(solution)/shard_map/ppermute | solution.py:400
  7.8 0.0 copy-start
  7.8 0.0 copy-start.1
  7.8 26.8 %all_to_all.15.in_ref = f32[16,4,128]{2,1,0:T(4,128)S(1)} all-to-all(f32[16,4,128]{2,1,0:T(4,128)S(1)} %get-tuple-element.11), channel_id=1, replica_groups={{10,11,14,15,6,7,8,9,2,12,3,13,4,5,0,1},{26,27,30,31,22,23,24,25,18,28,..., dimensions={0} | all-to-all | bytes 65536 | tf_op jit(solution)/shard_map/all_to_all | solution.py:399
  34.6 0.2 shard_map.87.panel_ref
  34.9 30.1 %all_to_all.16.panels_ref = f32[16,16,256]{2,1,0:T(8,128)S(1)} all-to-all(f32[16,16,256]{2,1,0:T(8,128)S(1)} %broadcast_in_dim.2), channel_id=1, replica_groups={{256,352,448,32,128,224,320,416,0,96,192,288,384,480,64,160},{257,353,4..., dimensions={0} | all-to-all | bytes 524288 | tf_op jit(solution)/shard_map/all_to_all | solution.py:402
  65.0 0.0 collective-permute-done.other_ref
  65.0 0.8 %shard_map.88 = f32[32,8,128]{2,1,0:T(8,128)S(1)} custom-call(s32[1]{0:T(128)} %bitcast.side_ref, f32[16,16,256]{2,1,0:T(8,128)S(1)} %all_to_all.16.panels_ref, f32[8,16,2,8,128]{4,3,2,1,0:T(8,128)S(1)} %get-tuple-element.13.mine_ref, f32[8,16,2,8,128]{4,3,2,1,0:T(8,128)S(1)} %collective-permute-done.other_ref, f32[16,256]{1,0:T(8,128)S(1)} %shard_map.87.panel_ref, ...), custom_call_target="tpu_custom_call" | custom-call | tf_op jit(solution)/shard_map/pallas_call | solution.py:341
  65.9 11.2 %all_to_all.17.in_ref = f32[32,8,128]{2,1,0:T(8,128)S(1)} all-to-all(f32[32,8,128]{2,1,0:T(8,128)S(1)} %shard_map.88), channel_id=1, replica_groups={{10,11,26,27,14,15,30,31,6,7,22,24,23,25,28,29,2,8,3,9,18,20,19,21,12,1..., dimensions={0} | all-to-all | bytes 262144 | tf_op jit(solution)/shard_map/all_to_all | solution.py:413
  77.1 0.0 copy-done
  77.1 0.0 copy-done.1
  77.1 1.9 %shard_map.89 = (f32[8,32,128]{2,1,0:T(8,128)}, f32[4,16]{1,0:T(4,128)}) custom-call(s32[1]{0:T(128)} %bitcast.side_ref, f32[32,8,128]{2,1,0:T(8,128)S(1)} %all_to_all.17.in_ref, f32[16,256]{1,0:T(8,128)S(1)} %shard_map.87.panel_ref, f32[1,512]{1,0:T(1,128)S(1)} %get-tuple-element.15.place_ref, bf16[256,512]{1,0:T(8,128)(2,1)S(1)} %get-tuple-element.16.whi_ref, ...), custom_call_target="tpu_custom_call" | custom-call | tf_op jit(solution)/shard_map/pallas_call | solution.py:341
  (1 shorter events, 0.0 us)
Async XLA Ops:
  3.8 61.3 %collective-permute-start = (f32[8,16,2,8,128]{4,3,2,1,0:T(8,128)}, f32[8,16,2,8,128]{4,3,2,1,0:T(8,128)S(1)}, u32[]{:S(2)}, u32[]{:S(2)}) collective-permute-start(f32[8,16,2,8,128]{4,3,2,1,0:T(8,128)} %get-tuple-element.14), channel_id=1, source_target_pairs={{0,16},{16,0},{1,17},{17,1},{2,18},{18,2},{3,19},{19,3},{4,20},{20... | collective-permute-start | bytes 3145736 | tf_op jit(solution)/shard_map/ppermute | solution.py:400
  7.8 69.3 %copy-start = (bf16[8,2,128,128]{3,2,1,0:T(8,128)(2,1)S(1)}, bf16[8,2,128,128]{3,2,1,0:T(8,128)(2,1)}, u32[]{:S(2)}) copy-start(bf16[8,2,128,128]{3,2,1,0:T(8,128)(2,1)} %inv_ref.1) | copy-start | bytes 1572868
  7.8 69.3 %copy-start.1 = (bf16[8,16,2,128]{3,2,1,0:T(2,128)(2,1)S(1)}, bf16[8,16,2,128]{3,2,1,0:T(2,128)(2,1)}, u32[]{:S(2)}) copy-start(bf16[8,16,2,128]{3,2,1,0:T(2,128)(2,1)} %param.7) | copy-start | bytes 196612

commit v6 on v5

--- a/solution.py
+++ b/solution.py
@@ -312,9 +312,9 @@
 
 POOL = "yl"
 GATHER = "z"
-LEVELS = (8, 11, 14, 1, 4, 7, 10, 13, 0, 3, 6, 9, 12, 15, 2, 5)
-FIRST = (10, 11, 14, 15, 6, 7, 8, 9, 2, 12, 3, 13, 4, 5, 0, 1)
-LAST = (10, 11, 26, 27, 14, 15, 30, 31, 6, 7, 22, 24, 23, 25, 28, 29, 2, 8, 3, 9, 18, 20, 19, 21, 12, 13, 4, 5, 16, 17, 0, 1)
+LEVELS = (8, 5, 2, 15, 12, 9, 6, 3, 0, 13, 10, 7, 4, 1, 14, 11)
+FIRST = (10, 11, 6, 7, 14, 15, 8, 9, 2, 4, 3, 5, 12, 13, 0, 1)
+LAST = (10, 11, 26, 27, 6, 7, 22, 23, 14, 24, 15, 25, 30, 31, 20, 21, 2, 8, 3, 9, 18, 19, 4, 28, 5, 29, 12, 16, 13, 17, 0, 1)
 VMEM = pltpu.VMEM
 
 

time: 79.2 us -> 79.5 us (level)
  no operation moved by 1% of the time
where the time goes in v6:
time: 79.5 us; the launch traced here: 79.2 us
  blocking collectives  68.4 us (86%)
  Pallas kernels  6.08 us (8%)
  starting transfers between devices  4.02 us (5%)
    all_to_all x1, blocking collectives, per_device(): lax.all_to_all(jnp.broadcast_to(panel[None], (levels, species, slots)), G...  30.3 us
    all_to_all x1, blocking collectives, per_device(): lax.all_to_all(outgoing, SUB, 0, 0, axis_index_groups=[list(FIRST)])  26.8 us
    all_to_all x1, blocking collectives, per_device(): lax.all_to_all(partial, (POOL,) + SUB, 0, 0, axis_index_groups=[list(LAST)])  11.3 us
    pallas_call x4, Pallas kernels, call(): pl.pallas_call(kernel, out_shape=outs, in_specs=[pl.BlockSpec(memory_spac...  6.08 us
    ppermute x1, starting transfers between devices, per_device(): other = lax.ppermute(away, POOL, [(0, 1), (1, 0)])  4.02 us
  transfers between devices with their start and end apart: 1, of which 0 were waited for; matrix products, arithmetic and copies ran while one was open for 0% of the time, Pallas kernels for 0%

profile of v6, /device:TPU:1, one launch (start us, length us, event | category | flops | bytes accessed | tf_op | source)
XLA Modules:
  0.0 79.2 jit_solution(5265252554527142081)
XLA Ops:
  0.6 3.1 %shard_map.86 = (f32[16,4,128]{2,1,0:T(4,128)S(1)}, f32[1,512]{1,0:T(1,128)S(1)}, bf16[256,512]{1,0:T(8,128)(2,1)S(1)}, bf16[256,512]{1,0:T(8,128)(2,1)S(1)}, bf...) custom-call(s32[1]{0:T(128)} %bitcast.1.own_ref, s32[1]{0:T(128)} %bitcast.side_ref, ...), custom_call_target="tpu_custom_call" | custom-call | tf_op jit(solution)/shard_map/pallas_call | solution.py:341
  3.8 4.0 %collective-permute-start = (f32[8,16,2,8,128]{4,3,2,1,0:T(8,128)}, f32[8,16,2,8,128]{4,3,2,1,0:T(8,128)S(1)}, u32[]{:S(2)}, u32[]{:S(2)}) collective-permute-start(f32[8,16,2,8,128]{4,3,2,1,0:T(8,128)} %get-tuple-element.14), channel_id=1, source_target_pairs={{0,16},{16,0},{1,17},{17,1},{2,18},{18,2},{3,19},{19,3},{4,20},{20... | collective-permute-start | bytes 3145736 | tf_op jit(solution)/shard_map/ppermute | solution.py:400
  7.8 0.0 copy-start
  7.8 0.0 copy-start.1
  7.8 26.8 %all_to_all.15.in_ref = f32[16,4,128]{2,1,0:T(4,128)S(1)} all-to-all(f32[16,4,128]{2,1,0:T(4,128)S(1)} %get-tuple-element.11), channel_id=1, replica_groups={{10,11,6,7,14,15,8,9,2,4,3,5,12,13,0,1},{26,27,22,23,30,31,24,25,18,20,..., dimensions={0} | all-to-all | bytes 65536 | tf_op jit(solution)/shard_map/all_to_all | solution.py:399
  34.6 0.2 shard_map.87.panel_ref
  34.9 30.3 %all_to_all.16.panels_ref = f32[16,16,256]{2,1,0:T(8,128)S(1)} all-to-all(f32[16,16,256]{2,1,0:T(8,128)S(1)} %broadcast_in_dim.2), channel_id=1, replica_groups={{256,160,64,480,384,288,192,96,0,416,320,224,128,32,448,352},{257,161,6..., dimensions={0} | all-to-all | bytes 524288 | tf_op jit(solution)/shard_map/all_to_all | solution.py:402
  65.2 0.0 collective-permute-done.other_ref
  65.2 0.8 %shard_map.88 = f32[32,8,128]{2,1,0:T(8,128)S(1)} custom-call(s32[1]{0:T(128)} %bitcast.side_ref, f32[16,16,256]{2,1,0:T(8,128)S(1)} %all_to_all.16.panels_ref, f32[8,16,2,8,128]{4,3,2,1,0:T(8,128)S(1)} %get-tuple-element.13.mine_ref, f32[8,16,2,8,128]{4,3,2,1,0:T(8,128)S(1)} %collective-permute-done.other_ref, f32[16,256]{1,0:T(8,128)S(1)} %shard_map.87.panel_ref, ...), custom_call_target="tpu_custom_call" | custom-call | tf_op jit(solution)/shard_map/pallas_call | solution.py:341
  66.0 11.3 %all_to_all.17.in_ref = f32[32,8,128]{2,1,0:T(8,128)S(1)} all-to-all(f32[32,8,128]{2,1,0:T(8,128)S(1)} %shard_map.88), channel_id=1, replica_groups={{10,11,26,27,6,7,22,23,14,24,15,25,30,31,20,21,2,8,3,9,18,19,4,28,5,29,..., dimensions={0} | all-to-all | bytes 262144 | tf_op jit(solution)/shard_map/all_to_all | solution.py:413
  77.3 0.0 copy-done
  77.3 0.0 copy-done.1
  77.3 1.9 %shard_map.89 = (f32[8,32,128]{2,1,0:T(8,128)}, f32[4,16]{1,0:T(4,128)}) custom-call(s32[1]{0:T(128)} %bitcast.side_ref, f32[32,8,128]{2,1,0:T(8,128)S(1)} %all_to_all.17.in_ref, f32[16,256]{1,0:T(8,128)S(1)} %shard_map.87.panel_ref, f32[1,512]{1,0:T(1,128)S(1)} %get-tuple-element.15.place_ref, bf16[256,512]{1,0:T(8,128)(2,1)S(1)} %get-tuple-element.16.whi_ref, ...), custom_call_target="tpu_custom_call" | custom-call | tf_op jit(solution)/shard_map/pallas_call | solution.py:341
  (1 shorter events, 0.0 us)
Async XLA Ops:
  3.8 61.4 %collective-permute-start = (f32[8,16,2,8,128]{4,3,2,1,0:T(8,128)}, f32[8,16,2,8,128]{4,3,2,1,0:T(8,128)S(1)}, u32[]{:S(2)}, u32[]{:S(2)}) collective-permute-start(f32[8,16,2,8,128]{4,3,2,1,0:T(8,128)} %get-tuple-element.14), channel_id=1, source_target_pairs={{0,16},{16,0},{1,17},{17,1},{2,18},{18,2},{3,19},{19,3},{4,20},{20... | collective-permute-start | bytes 3145736 | tf_op jit(solution)/shard_map/ppermute | solution.py:400
  7.8 69.5 %copy-start = (bf16[8,2,128,128]{3,2,1,0:T(8,128)(2,1)S(1)}, bf16[8,2,128,128]{3,2,1,0:T(8,128)(2,1)}, u32[]{:S(2)}) copy-start(bf16[8,2,128,128]{3,2,1,0:T(8,128)(2,1)} %inv_ref.1) | copy-start | bytes 1572868
  7.8 69.5 %copy-start.1 = (bf16[8,16,2,128]{3,2,1,0:T(2,128)(2,1)S(1)}, bf16[8,16,2,128]{3,2,1,0:T(2,128)(2,1)}, u32[]{:S(2)}) copy-start(bf16[8,16,2,128]{3,2,1,0:T(2,128)(2,1)} %param.7) | copy-start | bytes 196612
